TPU v7x, 32 devices: a whole 2x2x4 slice. The times are simulated.
32 devices in a mesh: dp: 8 (over y, x, core), tensor: 4 (over z).
Axes of the slice: x: 2, y: 2, z: 4, core: 2. Of those that a mesh axis runs over, the one named last changes fastest.
Arguments:
- prefill_states: bfloat16 [64, 2, 64, 128, 128], P('dp', None, 'tensor'), may hold values from -6 to 6
- prompt_slot: int32 [64], replicated, may hold values from 0 to 63, as said below
- sample_prompt: int32 [1024], P('dp'), may hold values from 0 to 63, as said below
- queries: bfloat16 [1024, 2, 2, 8192], P('dp', None, None, 'tensor'), may hold values from -2 to 2
- keys: bfloat16 [1024, 2, 2, 8192], P('dp', None, None, 'tensor'), may hold values from -3 to 3
- values: bfloat16 [1024, 2, 2, 8192], P('dp', None, None, 'tensor'), may hold values from -6 to 6
- gates: bfloat16 [1024, 2, 2, 8192], P('dp', None, None, 'tensor'), may hold values from -6 to 6
- norm_gain: float32 [2, 8192], P(None, 'tensor'), may hold values from 0.25 to 1.75
- decay_rate: float32 [2, 64], P(None, 'tensor'), may hold values from 0.01 to 1
Outputs:
- attended: float32 [1024, 2, 2, 8192], P('dp', None, None, 'tensor')
Inputs may be any that keep to these rules, and one draw needn't show every extreme that they name: `prompt_slot`: A permutation: each slot holds one prompt; slot s lies with dp group s // 8. `sample_prompt`: rows g * 128 to (g + 1) * 128 - 1 hold, for r = 0 to 3, exactly 4 rows of each prompt whose slot lies with group (g - r * 2) modulo 64 / 8, in any order.
All inputs are finite; a program needn't handle non-finite values.
Results may differ from a plain program's by a relative error of at most 0.0003.
Values may be sent and summed in bfloat16 or wider, within the bound.
No kernel may reach another device: no remote copies, remote signals or barrier semaphores. Data moves between devices by JAX's collectives and lax.ppermute only.
A program may use at most 64 MiB of HBM per device.

v0:
```python
import jax
import jax.numpy as jnp
from jax import lax
from jax.sharding import PartitionSpec as P

HEADS = 64
HEAD_DIM = 128


def shifted(block, axis, distance):
    devices = range(lax.axis_size(axis))
    route = [((i - distance) % len(devices), i) for i in devices]
    return lax.ppermute(block, axis, route)


def against(query_block, states):
    return jnp.einsum(
        "psjlhd,plhde->psjlhe", query_block, states, preferred_element_type=jnp.float32
    )


def local(
    prefill_states, prompt_slot, sample_prompt, queries, keys, values, gates, norm_gain, decay_rate
):
    group = lax.axis_index("dp")
    groups = lax.axis_size("dp")
    quarter = groups // 4
    owned = prefill_states.shape[0]
    rows = sample_prompt.shape[0]
    steps = queries.shape[1]
    layers = decay_rate.shape[0]
    local_heads = decay_rate.shape[1]
    width = queries.shape[3] // local_heads
    per_prompt = rows // (4 * owned)
    prompt_count = prompt_slot.shape[0]
    match = sample_prompt[:, None] == jnp.arange(prompt_count, dtype=jnp.int32)[None, :]
    slots = jnp.sum(jnp.where(match, prompt_slot[None, :], 0), axis=1)
    owner = slots // owned
    within = slots % owned
    reach = (group - owner) % groups // quarter
    candidate = reach * owned + within
    order = jnp.argsort(candidate * rows + jnp.arange(rows, dtype=jnp.int32))
    inverse = jnp.argsort(order)
    sorted_queries = queries[order].reshape(4, owned, per_prompt, steps, layers, local_heads, width)
    results = [against(sorted_queries[0], prefill_states)]
    for stride in range(1, 4):
        arrived = shifted(sorted_queries[stride], "dp", groups - stride * quarter)
        answer = against(arrived, prefill_states)
        results.append(shifted(answer, "dp", stride * quarter))
    products = jnp.stack(results)
    products = products.reshape(rows, steps, layers, local_heads, width)[inverse]
    retain = jnp.exp(-decay_rate)[None, :, :, None]
    shape = (rows, steps, layers, local_heads, width)
    query_all = queries.reshape(shape)
    key_all = keys.reshape(shape)
    value_all = values.reshape(shape)
    first_first = jnp.einsum(
        "slhd,slhd->slh", query_all[:, 0], key_all[:, 0], preferred_element_type=jnp.float32
    )[..., None]
    second_first = jnp.einsum(
        "slhd,slhd->slh", query_all[:, 1], key_all[:, 0], preferred_element_type=jnp.float32
    )[..., None]
    second_second = jnp.einsum(
        "slhd,slhd->slh", query_all[:, 1], key_all[:, 1], preferred_element_type=jnp.float32
    )[..., None]
    value_one = value_all[:, 0].astype(jnp.float32)
    value_two = value_all[:, 1].astype(jnp.float32)
    out_one = retain * products[:, 0] + first_first * value_one
    out_two = (
        retain * retain * products[:, 1]
        + retain * second_first * value_one
        + second_second * value_two
    )
    mixed = jnp.stack([out_one, out_two], axis=1).reshape(rows, steps, layers, local_heads * width)
    total = lax.psum(jnp.sum(mixed * mixed, axis=-1), "tensor")
    scale = lax.rsqrt(total / (HEADS * HEAD_DIM) + 1e-05)
    return (
        mixed * scale[..., None] * norm_gain[None, None] * jax.nn.sigmoid(gates.astype(jnp.float32))
    )


def solution(mesh):
    return jax.shard_map(
        local,
        mesh=mesh,
        in_specs=(
            P("dp", None, "tensor", None, None),
            P(),
            P("dp"),
            P("dp", None, None, "tensor"),
            P("dp", None, None, "tensor"),
            P("dp", None, None, "tensor"),
            P("dp", None, None, "tensor"),
            P(None, "tensor"),
            P(None, "tensor"),
        ),
        out_specs=P("dp", None, None, "tensor"),
        check_vma=False,
    )
```

profile of v0, /device:TPU:0, one launch (start us, length us, event | category | flops | bytes accessed | tf_op | source)
XLA Modules:
  0.0 152.6 jit_solution(4799387620769998287)
XLA Ops:
  0.0 0.8 select_reduce_fusion
  0.8 2.5 %sort.31 = (s32[128]{0:T(128)}, s32[128]{0:T(128)S(1)}) sort(s32[128]{0:T(128)S(1)} %iota_add_fusion, s32[128]{0:T(128)S(1)} %iota.15), dimensions={0}, to_apply=%region_1.2 | sort | flops 896 | bytes 2048 | tf_op jit(solution)/shard_map/jit(argsort)/sort | solution.py:42
  3.4 9.2 %gather_fusion = bf16[128,2,2,2048]{3,2,1,0:T(2,128)(2,1)S(1)} fusion(bf16[128,2,2,2048]{3,2,1,0:T(2,128)(2,1)} %param.12, s32[1024]{0:T(1024)S(1)} %pad_clamp_fusion.1), kind=kCustom, calls=%fused_computation | custom fusion | bytes 4194816 | tf_op jit(solution)/shard_map/gather | solution.py:44
  12.5 2.9 %fusion.30 = (bf16[32,2,2,2048]{3,2,1,0:T(2,128)(2,1)S(1)}, bf16[32,2,2,2048]{3,2,1,0:T(2,128)(2,1)}, bf16[32,2,2,2048]{3,2,1,0:T(2,128)(2,1)}, bf16[32,2,2,2048]{3,2,1,0:T(2,128)(2,1)S(1)}) fusion(bf16[128,2,2,2048]{3,2,1,0:T(2,128)(2,1)S(1)} %gather_fusion), kind=kLoop, calls=%fused_computation.61 | loop fusion | bytes 4194304 | tf_op jit(solution)/shard_map/slice | solution.py:45
  15.5 0.3 reshape.71
  15.8 1.2 copy.53
  17.0 3.0 %collective-permute-start.4 = (bf16[8,4,2,2,16,128]{5,1,2,4,3,0:T(4,128)(2,1)}, bf16[8,4,2,2,16,128]{5,1,2,4,3,0:T(4,128)(2,1)}, u32[]{:S(2)}, u32[]{:S(2)}) collective-permute-start(bf16[8,4,2,2,16,128]{5,1,2,4,3,0:T(4,128)(2,1)} %copy.53), channel_id=1, source_target_pairs={{24,0},{28,4},{0,8},{4,12},{8,16},{12,20},{16,24},{20,28},{25,1},{... | collective-permute-start | bytes 1572872 | tf_op jit(solution)/shard_map/ppermute | solution.py:13
  20.0 0.0 copy-start
  20.0 1.5 reshape.69
  21.5 1.2 copy.49
  22.7 1.0 collective-permute-start
  23.7 1.4 reshape.70
  25.1 1.2 copy.51
  26.3 2.0 %collective-permute-start.2 = (bf16[8,4,2,2,16,128]{5,1,2,4,3,0:T(4,128)(2,1)}, bf16[8,4,2,2,16,128]{5,1,2,4,3,0:T(4,128)(2,1)S(1)}, u32[]{:S(2)}, u32[]{:S(2)}) collective-permute-start(bf16[8,4,2,2,16,128]{5,1,2,4,3,0:T(4,128)(2,1)} %copy.51), channel_id=1, source_target_pairs={{16,0},{20,4},{24,8},{28,12},{0,16},{4,20},{8,24},{12,28},{17,1},{... | collective-permute-start | bytes 1572872 | tf_op jit(solution)/shard_map/ppermute | solution.py:13
  28.3 0.0 copy-done
  28.3 2.6 %reshape.37 = bf16[128,2,2,16,128]{4,3,2,1,0:T(8,128)(2,1)} reshape(bf16[128,2,2,2048]{3,2,1,0:T(2,128)(2,1)S(1)} %copy-done) | data formatting | bytes 4194304 | tf_op jit(solution)/shard_map/reshape | solution.py:54
  30.9 2.6 %sort.32 = (s32[128]{0:T(128)}, s32[128]{0:T(128)S(1)}) sort(s32[128]{0:T(128)S(1)} %get-tuple-element.7, s32[128]{0:T(128)S(1)} %iota.16), dimensions={0}, to_apply=%region_2.3 | sort | flops 896 | bytes 2048 | tf_op jit(solution)/shard_map/jit(argsort)/sort | solution.py:43
  33.5 0.0 copy-start.1
  33.5 4.5 %reshape.38 = bf16[128,2,2,16,128]{4,3,2,1,0:T(8,128)(2,1)} reshape(bf16[128,2,2,2048]{3,2,1,0:T(2,128)(2,1)} %param.13) | data formatting | bytes 4194304 | tf_op jit(solution)/shard_map/reshape | solution.py:55
  38.0 0.0 copy-done.1
  38.0 0.0 slice-start
  38.0 3.6 %fusion.11 = (f32[128,2,16]{2,1,0:T(2,128)S(1)}, f32[128,2,16]{2,1,0:T(2,128)S(1)}, f32[128,2,16]{2,1,0:T(2,128)S(1)}) fusion(bf16[128,2,2,16,128]{4,3,2,1,0:T(8,128)(2,1)S(1)} %copy-done.1, bf16[128,2,2,16,128]{4,3,2,1,0:T(8,128)(2,1)} %reshape.38), kind=kLoop, calls=%fused_computation.22 | loop fusion | flops 5230592 | bytes 4243456 | tf_op jit(solution)/shard_map/slhd,slhd->slh/dot_general | solution.py:57
  41.7 0.0 slice-start.1
  41.7 0.0 collective-permute-done.4
  41.7 6.9 %fusion.23 = f32[8,4,2,2,16,128]{5,1,2,4,3,0:T(4,128)} fusion(bf16[8,4,2,2,16,128]{5,1,2,4,3,0:T(4,128)(2,1)} %collective-permute-done.4, bf16[8,2,16,128,128]{4,3,2,1,0:T(8,128)(2,1)} %param.9), kind=kOutput, calls=%fused_computation.30 | convolution fusion | flops 67108864 | bytes 9961472 | tf_op jit(solution)/shard_map/psjlhd,plhde->psjlhe/dot_general | solution.py:17
  48.6 0.5 collective-permute-start.5
  49.2 0.0 collective-permute-done
  49.2 6.8 %fusion.17 = f32[8,4,2,2,16,128]{5,1,2,4,3,0:T(4,128)} fusion(bf16[8,4,2,2,16,128]{5,1,2,4,3,0:T(4,128)(2,1)} %collective-permute-done, bf16[8,2,16,128,128]{4,3,2,1,0:T(8,128)(2,1)} %param.9), kind=kOutput, calls=%fused_computation.28 | convolution fusion | flops 67108864 | bytes 9961472 | tf_op jit(solution)/shard_map/psjlhd,plhde->psjlhe/dot_general | solution.py:17
  56.0 1.5 collective-permute-start.1
  57.5 0.0 collective-permute-done.2
  57.5 0.0 slice-done
  57.5 0.0 slice-done.1
  57.5 3.3 %fusion.20 = f32[8,4,2,2,16,128]{5,1,2,4,3,0:T(4,128)} fusion(bf16[8,4,2,2,16,128]{5,1,2,4,3,0:T(4,128)(2,1)S(1)} %collective-permute-done.2, bf16[8,2,16,128,128]{4,3,2,1,0:T(8,128)(2,1)S(1)} %bitcast.66), kind=kOutput, calls=%fused_computation.29 | convolution fusion | flops 67108864 | bytes 9961472 | tf_op jit(solution)/shard_map/psjlhd,plhde->psjlhe/dot_general | solution.py:17
  60.8 0.0 collective-permute-start.3
  60.8 0.3 reshape.68
  61.2 0.0 copy-start.3
  61.2 3.2 %reshape.39 = bf16[128,2,2,16,128]{4,3,2,1,0:T(8,128)(2,1)S(1)} reshape(bf16[128,2,2,2048]{3,2,1,0:T(2,128)(2,1)} %param.14) | data formatting | bytes 4194304 | tf_op jit(solution)/shard_map/reshape | solution.py:56
  64.4 0.0 copy-done.3
  64.4 5.7 %fusion.14 = f32[1,8,4,2,2,16,128]{6,2,3,5,4,1,0:T(4,128)S(1)} fusion(bf16[8,2,16,128,128]{4,3,2,1,0:T(8,128)(2,1)} %param.9, bf16[8,4,2,2,16,128]{5,4,3,2,1,0:T(8,128)(2,1)S(1)} %reshape.68), kind=kOutput, calls=%fused_computation.27 | convolution fusion | flops 67108864 | bytes 9961472 | tf_op jit(solution)/shard_map/psjlhd,plhde->psjlhe/dot_general | solution.py:17
  70.1 4.9 %collective-permute-done.5 = f32[8,4,2,2,16,128]{5,1,2,4,3,0:T(4,128)} collective-permute-done((f32[8,4,2,2,16,128]{5,1,2,4,3,0:T(4,128)}, f32[8,4,2,2,16,128]{5,1,2,4,3,0:T(4,128)}, u32[]{:S(2)}, u32[]{:S(2)}) %collective-permute-start.5) | collective-permute-done | bytes 1048608 | tf_op jit(solution)/shard_map/ppermute | solution.py:13
  75.0 20.3 %collective-permute-done.1 = f32[8,4,2,2,16,128]{5,1,2,4,3,0:T(4,128)} collective-permute-done((f32[8,4,2,2,16,128]{5,1,2,4,3,0:T(4,128)}, f32[8,4,2,2,16,128]{5,1,2,4,3,0:T(4,128)}, u32[]{:S(2)}, u32[]{:S(2)}) %collective-permute-start.1) | collective-permute-done | bytes 1048608 | tf_op jit(solution)/shard_map/ppermute | solution.py:13
  95.3 11.7 %collective-permute-done.3 = f32[8,4,2,2,16,128]{5,1,2,4,3,0:T(4,128)} collective-permute-done((f32[8,4,2,2,16,128]{5,1,2,4,3,0:T(4,128)}, f32[8,4,2,2,16,128]{5,1,2,4,3,0:T(4,128)}, u32[]{:S(2)}, u32[]{:S(2)}) %collective-permute-start.3) | collective-permute-done | bytes 1048608 | tf_op jit(solution)/shard_map/ppermute | solution.py:13
  107.1 2.5 %pad_maximum_fusion = f32[4,8,4,2,2,16,128]{6,2,3,5,4,1,0:T(4,128)S(1)} fusion(f32[1,8,4,2,2,16,128]{6,2,3,5,4,1,0:T(4,128)} %bitcast.10, f32[1,8,4,2,2,16,128]{6,2,3,5,4,1,0:T(4,128)} %bitcast.8, f32[1,8,4,2,2,16,128]{6,2,3,5,4,1,0:T(4,128)} %bitcast.6, f32[1,8,4,2,2,16,128]{6,2,3,5,4,1,0:T(4,128)S(1)} %fusion.14), kind=kLoop, calls=%fused_computation.11 | loop fusion | flops 3145728 | bytes 8388608 | tf_op jit(solution)/shard_map/stack | solution.py:50
  109.6 2.8 %copy.54 = f32[4,8,4,2,2,16,128]{6,5,4,3,2,1,0:T(8,128)} copy(f32[4,8,4,2,2,16,128]{6,2,3,5,4,1,0:T(4,128)S(1)} %pad_maximum_fusion) | data formatting | bytes 8388608 | tf_op jit(solution)/shard_map/stack | solution.py:50
  112.4 4.9 %gather_fusion.1 = f32[128,2,2,16,128]{4,3,2,1,0:T(8,128)} fusion(f32[128,2,2,16,128]{4,3,2,1,0:T(8,128)} %bitcast.71, s32[1024]{0:T(1024)S(1)} %pad_clamp_fusion), kind=kCustom, calls=%fused_computation.1 | custom fusion | bytes 8389120 | tf_op jit(solution)/shard_map/gather | solution.py:51
  117.3 5.7 %fusion.8 = (f32[128,1,2,16,128]{4,3,2,1,0:T(8,128)}, f32[128,1,2,16,128]{4,3,2,1,0:T(8,128)}) fusion(f32[128,2,2,16,128]{4,3,2,1,0:T(8,128)} %gather_fusion.1, f32[128,2,16]{2,1,0:T(2,128)S(1)} %get-tuple-element.9, f32[2,16]{1,0:T(2,128)S(1)} %get-tuple-element.19, bf16[128,2,2,16,128]{4,3,2,1,0:T(8,128)(2,1)S(1)} %reshape.39, ...), kind=kLoop, calls=%fused_computation.19 | loop fusion | flops 5242880 | bytes 10535168 | tf_op jit(solution)/shard_map/add | solution.py:68
  123.0 2.3 %stack.29 = f32[128,1,2,2048]{3,2,0,1:T(2,128)S(1)} reshape(f32[128,1,2,16,128]{4,3,2,1,0:T(8,128)} %get-tuple-element.12) | data formatting | bytes 4194304 | tf_op jit(solution)/shard_map/stack | solution.py:74
  125.3 3.4 %stack.30 = f32[128,1,2,2048]{3,2,0,1:T(2,128)} reshape(f32[128,1,2,16,128]{4,3,2,1,0:T(8,128)} %get-tuple-element.13) | data formatting | bytes 4194304 | tf_op jit(solution)/shard_map/stack | solution.py:74
  128.7 0.0 copy-start.2
  128.7 4.1 %multiply_reduce_fusion = f32[128,2,2]{2,1,0:T(2,128)S(1)} fusion(f32[128,1,2,2048]{3,2,1,0:T(2,128)} %bitcast.69, f32[128,1,2,2048]{3,2,1,0:T(2,128)S(1)} %bitcast.67), kind=kLoop, calls=%fused_computation.13 | loop fusion | flops 3145216 | bytes 4196352 | tf_op jit(solution)/shard_map/reduce_sum | solution.py:75
  132.7 0.1 copy.57
  132.8 11.9 %psum.7 = f32[128,2,2]{0,2,1:T(2,128)S(1)} all-reduce(f32[128,2,2]{0,2,1:T(2,128)S(1)} %copy.57), channel_id=1, replica_groups=mesh['dp'=8,'tensor'=4] {'tensor'}, use_global_device_ids=true, to_apply=%region_4.5 | all-reduce | flops 512 | bytes 4096 | tf_op jit(solution)/shard_map/psum | solution.py:75
  144.8 0.2 copy.58
  144.9 0.0 copy-done.2
  145.0 7.7 %divide_multiply_fusion = f32[128,2,2,2048]{3,2,1,0:T(2,128)} fusion(bf16[128,2,2,2048]{3,2,1,0:T(2,128)(2,1)} %param.15, f32[2,2048]{1,0:T(2,128)S(1)} %copy-done.2, f32[128,2,2]{2,1,0:T(2,128)S(1)} %copy.58, f32[128,1,2,2048]{3,2,1,0:T(2,128)} %bitcast.70, f32[128,1,2,2048]{3,2,1,0:T(2,128)S(1)} %bitcast.68), kind=kLoop, calls=%fused_computation.10 | loop fusion | flops 8388608 | bytes 10504192 | tf_op jit(solution)/shard_map/mul | solution.py:78
  (12 shorter events, 0.1 us)
Async XLA Ops:
  17.0 24.7 %collective-permute-start.4 = (bf16[8,4,2,2,16,128]{5,1,2,4,3,0:T(4,128)(2,1)}, bf16[8,4,2,2,16,128]{5,1,2,4,3,0:T(4,128)(2,1)}, u32[]{:S(2)}, u32[]{:S(2)}) collective-permute-start(bf16[8,4,2,2,16,128]{5,1,2,4,3,0:T(4,128)(2,1)} %copy.53), channel_id=1, source_target_pairs={{24,0},{28,4},{0,8},{4,12},{8,16},{12,20},{16,24},{20,28},{25,1},{... | collective-permute-start | bytes 1572872 | tf_op jit(solution)/shard_map/ppermute | solution.py:13
  20.0 8.3 %copy-start = (bf16[128,2,2,2048]{3,2,1,0:T(2,128)(2,1)S(1)}, bf16[128,2,2,2048]{3,2,1,0:T(2,128)(2,1)}, u32[]{:S(2)}) copy-start(bf16[128,2,2,2048]{3,2,1,0:T(2,128)(2,1)} %param.12) | copy-start | bytes 6291460
  22.7 26.5 %collective-permute-start = (bf16[8,4,2,2,16,128]{5,1,2,4,3,0:T(4,128)(2,1)}, bf16[8,4,2,2,16,128]{5,1,2,4,3,0:T(4,128)(2,1)}, u32[]{:S(2)}, u32[]{:S(2)}) collective-permute-start(bf16[8,4,2,2,16,128]{5,1,2,4,3,0:T(4,128)(2,1)} %copy.49), channel_id=1, source_target_pairs={{8,0},{12,4},{16,8},{20,12},{24,16},{28,20},{0,24},{4,28},{9,1},{1... | collective-permute-start | bytes 1572872 | tf_op jit(solution)/shard_map/ppermute | solution.py:13
  26.3 31.2 %collective-permute-start.2 = (bf16[8,4,2,2,16,128]{5,1,2,4,3,0:T(4,128)(2,1)}, bf16[8,4,2,2,16,128]{5,1,2,4,3,0:T(4,128)(2,1)S(1)}, u32[]{:S(2)}, u32[]{:S(2)}) collective-permute-start(bf16[8,4,2,2,16,128]{5,1,2,4,3,0:T(4,128)(2,1)} %copy.51), channel_id=1, source_target_pairs={{16,0},{20,4},{24,8},{28,12},{0,16},{4,20},{8,24},{12,28},{17,1},{... | collective-permute-start | bytes 1572872 | tf_op jit(solution)/shard_map/ppermute | solution.py:13
  33.5 4.5 %copy-start.1 = (bf16[128,2,2,16,128]{4,3,2,1,0:T(8,128)(2,1)S(1)}, bf16[128,2,2,16,128]{4,3,2,1,0:T(8,128)(2,1)}, u32[]{:S(2)}) copy-start(bf16[128,2,2,16,128]{4,3,2,1,0:T(8,128)(2,1)} %reshape.37) | copy-start | bytes 6291460
  38.0 19.5 %slice-start = ((s8[8388608]{0:T(1024)(128)(4,1)}), s8[4194304]{0:T(1024)(128)(4,1)S(1)}, s32[]{:S(2)}) async-start(s8[8388608]{0:T(1024)(128)(4,1)} %bitcast.65), calls=%async_computation | async-start | bytes 8388608
  41.7 15.8 %slice-start.1 = ((s8[8388608]{0:T(1024)(128)(4,1)}), s8[4194304]{0:T(1024)(128)(4,1)S(1)}, s32[]{:S(2)}) async-start(s8[8388608]{0:T(1024)(128)(4,1)} %bitcast.65), calls=%async_computation.1 | async-start | bytes 8388608
  48.6 26.4 %collective-permute-start.5 = (f32[8,4,2,2,16,128]{5,1,2,4,3,0:T(4,128)}, f32[8,4,2,2,16,128]{5,1,2,4,3,0:T(4,128)}, u32[]{:S(2)}, u32[]{:S(2)}) collective-permute-start(f32[8,4,2,2,16,128]{5,1,2,4,3,0:T(4,128)} %fusion.23), channel_id=1, source_target_pairs={{8,0},{12,4},{16,8},{20,12},{24,16},{28,20},{0,24},{4,28},{9,1},{1... | collective-permute-start | bytes 3145736 | tf_op jit(solution)/shard_map/ppermute | solution.py:13
  56.0 39.3 %collective-permute-start.1 = (f32[8,4,2,2,16,128]{5,1,2,4,3,0:T(4,128)}, f32[8,4,2,2,16,128]{5,1,2,4,3,0:T(4,128)}, u32[]{:S(2)}, u32[]{:S(2)}) collective-permute-start(f32[8,4,2,2,16,128]{5,1,2,4,3,0:T(4,128)} %fusion.17), channel_id=1, source_target_pairs={{24,0},{28,4},{0,8},{4,12},{8,16},{12,20},{16,24},{20,28},{25,1},{... | collective-permute-start | bytes 3145736 | tf_op jit(solution)/shard_map/ppermute | solution.py:13
  60.8 46.3 %collective-permute-start.3 = (f32[8,4,2,2,16,128]{5,1,2,4,3,0:T(4,128)}, f32[8,4,2,2,16,128]{5,1,2,4,3,0:T(4,128)}, u32[]{:S(2)}, u32[]{:S(2)}) collective-permute-start(f32[8,4,2,2,16,128]{5,1,2,4,3,0:T(4,128)} %fusion.20), channel_id=1, source_target_pairs={{16,0},{20,4},{24,8},{28,12},{0,16},{4,20},{8,24},{12,28},{17,1},{... | collective-permute-start | bytes 3145736 | tf_op jit(solution)/shard_map/ppermute | solution.py:13
  61.2 3.2 %copy-start.3 = (f32[2,16]{1,0:T(2,128)S(1)}, f32[2,16]{1,0:T(2,128)}, u32[]{:S(2)}) copy-start(f32[2,16]{1,0:T(2,128)} %param.17) | copy-start | bytes 388
  128.7 16.3 %copy-start.2 = (f32[2,2048]{1,0:T(2,128)S(1)}, f32[2,2048]{1,0:T(2,128)}, u32[]{:S(2)}) copy-start(f32[2,2048]{1,0:T(2,128)} %param.16) | copy-start | bytes 49156
where the time goes:
time: 153 us
  local copies, waits for them, and re-layouts  43.3 us (28%)
  waiting for transfers between devices  37 us (24%)
  other arithmetic  29.5 us (19%)
  matrix products  22.7 us (15%)
  blocking collectives  11.9 us (8%)
  starting transfers between devices  7.98 us (5%)
    ppermute x6, waiting for transfers between devices, shifted(): return lax.ppermute(block, axis, route)  37 us
    dot_general x4, matrix products, against(): jnp.einsum('psjlhd,plhde->psjlhe', query_block, states, preferred_element...  22.7 us
    psum x1, blocking collectives, local(): total = lax.psum(jnp.sum(mixed * mixed, axis=-1), 'tensor')  11.9 us
    gather x1, local copies, waits for them, and re-layouts, local(): queries[order]  9.19 us
    ppermute x6, starting transfers between devices, shifted(): return lax.ppermute(block, axis, route)  7.98 us
    mul x1, other arithmetic, local(): mixed * scale[..., None] * norm_gain[None, None]  7.66 us
    squeeze x6, local copies, waits for them, and re-layouts, local(): arrived = shifted(sorted_queries[stride], 'dp', groups - stride * quarter)  6.84 us
    another operation x2, local copies, waits for them, and re-layouts, local(): jnp.stack([out_one, out_two], axis=1)  5.69 us
  transfers between devices with their start and end apart: 6, of which 3 were waited for; matrix products, arithmetic and copies ran while one was open for 29% of the time, Pallas kernels for 0%

commit v1 on v0

v1 whole, which is shorter than its diff:
```python
import functools

import jax
import jax.numpy as jnp
from jax import lax
from jax.experimental import pallas as pl
from jax.experimental.pallas import tpu as pltpu
from jax.sharding import PartitionSpec as P

HEADS = 64
HEAD_DIM = 128
LANES = 128
ANY = pl.BlockSpec(memory_space=pl.ANY)
SMEM = pl.BlockSpec(memory_space=pltpu.SMEM)
VMEM = pl.BlockSpec(memory_space=pltpu.VMEM)
TOP = 32767.0
ROUND = 12582912.0


def params(mib):
    return pltpu.CompilerParams(vmem_limit_bytes=mib << 20)


def cost(flops, moved):
    return pl.CostEstimate(flops=flops, bytes_accessed=moved, transcendentals=0)


def rows_view(x):
    rows, steps, layers, columns = x.shape
    heads = columns // LANES
    x = x.reshape(rows, steps, layers, heads, LANES).transpose(0, 1, 3, 2, 4)
    return x.reshape(rows, steps * heads * layers, LANES)


def rows_unview(y, steps, layers):
    rows, lines, _ = y.shape
    heads = lines // (steps * layers)
    y = y.reshape(rows, steps, heads, layers, LANES).transpose(0, 1, 3, 2, 4)
    return y.reshape(rows, steps, layers, heads * LANES)


def iota(shape, axis):
    return lax.broadcasted_iota(jnp.int32, shape, axis)


def pack_rows(order_ref, first, prompts, q_ref, scratch, out_ref):
    lines = q_ref.shape[1]
    half = lines // 2
    total = out_ref.shape[1]
    samples = total // lines

    def body(p, carry):
        for c in range(samples):
            s = order_ref[0, first + p * samples + c]
            for j in range(2):
                block = q_ref[s, j * half : (j + 1) * half, :].astype(jnp.float32)
                scratch[p % 2, pl.ds(c * 2 + j, half, stride=2 * samples), :] = block
        out_ref[p] = scratch[p % 2].astype(jnp.bfloat16)
        return carry

    lax.fori_loop(0, prompts, body, 0, unroll=2)


def order_kernel(
    owned, quarter, chunks, place_ref, slot_ref, prompt_ref, q_hbm,
    order_ref, *rest,
):
    outs, (q_vmem, line, scratch, sems) = rest[: len(chunks)], rest[len(chunks) :]
    load = pltpu.make_async_copy(q_hbm, q_vmem, sems.at[0])
    load.start()
    rows = prompt_ref.shape[1]
    count = slot_ref.shape[1]
    per = rows // (4 * owned)
    f32 = jnp.float32
    slot = slot_ref[...]
    owner = lax.div(lax.div(slot, owned), quarter)
    table = ((owner ^ place_ref[0, 0]) * owned + lax.rem(slot, owned)).astype(f32)
    down, across = iota((rows, rows), 0), iota((rows, rows), 1)
    prompt = jnp.broadcast_to(prompt_ref[...].astype(f32), (rows, rows))
    prompt = jnp.sum(jnp.where(down == across, prompt, 0.0), axis=1, keepdims=True)
    hit = prompt == iota((rows, count), 1).astype(f32)
    key = jnp.sum(jnp.where(hit, jnp.broadcast_to(table, (rows, count)), 0.0), axis=1, keepdims=True)
    key_all = jnp.broadcast_to(key, (rows, rows))
    key_row = jnp.sum(jnp.where(down == across, key_all, 0.0), axis=0, keepdims=True)
    same = (key_all == jnp.broadcast_to(key_row, (rows, rows))) & (across < down)
    rank = jnp.sum(jnp.where(same, 1.0, 0.0), axis=1, keepdims=True)
    spot = key * per + rank
    found = jnp.broadcast_to(spot, (rows, rows)) == across.astype(f32)
    line[...] = jnp.sum(jnp.where(found, down.astype(f32), 0.0), axis=0, keepdims=True).astype(jnp.int32)
    note = pltpu.make_async_copy(line, order_ref, sems.at[1])
    note.start()
    note.wait()
    load.wait()
    for chunk, out_ref in zip(chunks, outs):
        pack_rows(order_ref, chunk * owned * per, owned, q_vmem, scratch, out_ref)


def pack_kernel(owned, per, chunks, order_ref, q_ref, *rest):
    outs, scratch = rest[:-1], rest[-1]
    for chunk, out_ref in zip(chunks, outs):
        pack_rows(order_ref, chunk * owned * per, owned, q_ref, scratch, out_ref)


def reach_kernel(coded, q_ref, s_ref, out_ref, *scratch):
    heads = s_ref.shape[2]
    lines = q_ref.shape[1]
    p = pl.program_id(0)
    first = p * lines if coded else 0

    def products(h):
        a = q_ref[0, h * 16 : (h + 1) * 16, :]
        w = jnp.concatenate([s_ref[0, 0, h], s_ref[0, 1, h]], axis=1)
        y = jnp.dot(a, w, preferred_element_type=jnp.float32)
        return y[:8, :LANES], y[8:, LANES:]

    if not coded:
        for h in range(heads):
            for l, r in enumerate(products(h)):
                at = h * 16 + l * 8
                out_ref[0, at : at + 8, :] = r
        return
    exact, power = scratch
    lane = iota((8, LANES), 1)
    base = (p // 2) * 2 * heads
    peak = jnp.ones((8, LANES), jnp.float32)
    for h in range(heads):
        for l, r in enumerate(products(h)):
            at = h * 16 + l * 8
            exact[at : at + 8, :] = r
            top = jnp.max(jnp.abs(r), axis=1, keepdims=True)
            peak = jnp.where(lane == h * 2 + l, top, peak)
    e = jnp.ceil(jnp.log2(jnp.maximum(peak, 1e-32)) + 1e-4)
    factor = jnp.exp2(15.0 - e) * (TOP / 32768.0)
    row = pl.multiple_of((p % 2) * 8, 8)
    mine = (lane >= base) & (lane < base + 2 * heads)
    spread = jnp.concatenate([e[:, : 2 * heads]] * (LANES // (2 * heads)), axis=1)
    power[pl.ds(row, 8), :] = jnp.where(mine, spread, power[pl.ds(row, 8), :])
    for h in range(heads):
        code = []
        for l in range(2):
            at = h * 16 + l * 8
            f = jnp.broadcast_to(factor[:, h * 2 + l : h * 2 + l + 1], (8, LANES))
            code.append((exact[at : at + 8, :] * f + ROUND) - ROUND)
        code = jnp.concatenate(code, axis=0).astype(jnp.int32).astype(jnp.int16)
        out_ref[pl.ds(pl.multiple_of(first + h * 16, 16), 16), :] = code

    @pl.when(p == pl.num_programs(0) - 1)
    def _():
        tail = pl.num_programs(0) * lines
        out_ref[pl.ds(pl.multiple_of(tail, 16), 16), :] = power[...].astype(jnp.int32).astype(jnp.int16)


def reach(query, states, first, prompts, coded):
    _, lines, _ = query.shape
    _, layers, heads, _, _ = states.shape
    if coded:
        shape = jax.ShapeDtypeStruct((prompts * lines + 16, LANES), jnp.int16)
        scratch = [pltpu.VMEM((lines, LANES), jnp.float32), pltpu.VMEM((16, LANES), jnp.float32)]
        out = pl.BlockSpec(shape.shape, lambda p: (0, 0))
    else:
        shape = jax.ShapeDtypeStruct((prompts, lines, LANES), jnp.float32)
        out = pl.BlockSpec((1, lines, LANES), lambda p: (p, 0, 0))
        scratch = []
    return pl.pallas_call(
        functools.partial(reach_kernel, coded),
        grid=(prompts,),
        in_specs=[
            pl.BlockSpec((1, lines, LANES), lambda p: (first + p, 0, 0)),
            pl.BlockSpec((1, layers, heads, LANES, LANES), lambda p: (first + p, 0, 0, 0, 0)),
        ],
        out_specs=out,
        out_shape=shape,
        scratch_shapes=scratch,
        compiler_params=params(24),
        cost_estimate=cost(prompts * lines * LANES * LANES * 4, prompts * layers * heads * LANES * LANES * 2),
        name="reach",
    )(query, states)


def prepare_kernel(block, order_ref, q_ref, k_ref, v_ref, g_ref, retain_ref, gain_ref, own_ref, gate_ref):
    half = q_ref.shape[1] // 2
    first = pl.program_id(0) * block
    retain, gain = retain_ref[...], gain_ref[...]
    f32 = jnp.float32

    def body(i, carry):
        s = order_ref[0, first + i]
        one, two = slice(0, half), slice(half, 2 * half)
        q1, q2 = q_ref[s, one, :].astype(f32), q_ref[s, two, :].astype(f32)
        k1, k2 = k_ref[s, one, :].astype(f32), k_ref[s, two, :].astype(f32)
        v1, v2 = v_ref[s, one, :].astype(f32), v_ref[s, two, :].astype(f32)
        first_first = jnp.sum(q1 * k1, axis=1, keepdims=True)
        second_first = jnp.sum(q2 * k1, axis=1, keepdims=True)
        second_second = jnp.sum(q2 * k2, axis=1, keepdims=True)
        own_ref[i, one, :] = first_first * v1
        own_ref[i, two, :] = retain * second_first * v1 + second_second * v2
        gate_ref[i, one, :] = gain * jax.nn.sigmoid(g_ref[s, one, :].astype(f32))
        gate_ref[i, two, :] = gain * jax.nn.sigmoid(g_ref[s, two, :].astype(f32))
        return carry

    lax.fori_loop(0, block, body, 0, unroll=2)


def combine_kernel(coded, first, *refs):
    if coded:
        code_ref, power_ref, own_ref, gate_ref, retain_ref, sum_in, out_ref, sum_ref, exact = refs
    else:
        code_ref, own_ref, gate_ref, retain_ref, sum_in, out_ref, sum_ref = refs
    samples, lines, _ = own_ref.shape
    half = lines // 2
    p = pl.program_id(0)
    lane = iota((8, LANES), 1)
    if coded:
        row = pl.multiple_of((p % 2) * 8, 8)
        power = power_ref[...].astype(jnp.int32).astype(jnp.float32)
        power = jnp.where(p % 2 == 0, power[:8], power[8:])
        unit = jnp.exp2(power - 15.0) * (32768.0 / TOP)
        unit = pltpu.roll(unit, lax.rem(LANES - (p // 2) * half, LANES), 1)
        for h in range(half // 2):
            code = code_ref[h * 16 : (h + 1) * 16, :].astype(jnp.int32).astype(jnp.float32)
            for l in range(2):
                at = h * 16 + l * 8
                u = jnp.broadcast_to(unit[:, h * 2 + l : h * 2 + l + 1], (8, LANES))
                exact[at : at + 8, :] = code[l * 8 : l * 8 + 8] * u
        reached = exact
    else:
        reached = code_ref.at[0]

    @pl.when(p == 0)
    def _():
        sum_ref[...] = jnp.zeros_like(sum_ref)

    retain = retain_ref[...]
    squared = retain * retain
    totals = [sum_ref[:8], sum_ref[8:]]
    for c in range(samples):
        for j in range(2):
            at = slice(j * half, (j + 1) * half)
            r = reached[pl.ds(c * 2 + j, half, stride=2 * samples), :]
            mixed = (squared if j else retain) * r + own_ref[c, at, :]
            out_ref[c, at, :] = mixed * gate_ref[c, at, :]
            power = jnp.sum((mixed * mixed).reshape(half // 8, 8, LANES), axis=0)
            power = jnp.sum(power, axis=1, keepdims=True)
            totals[j] = jnp.where(lane == first + p * samples + c, power, totals[j])
    sum_ref[:8] = totals[0]
    sum_ref[8:] = totals[1]

    @pl.when(p == pl.num_programs(0) - 1)
    def _():
        for j in range(2):
            t = sum_ref[j * 8 : j * 8 + 8]
            u = t + pltpu.roll(t, 4, 0)
            sum_ref[j * 8 : j * 8 + 8] = u + pltpu.roll(u, 2, 0) + sum_in[j * 8 : j * 8 + 8]


def combine(coded, products, own, gate, retain, sums, start, prompts, first):
    lines = own.shape[1]
    total = products.shape[1] if not coded else (products.shape[0] - 16) // prompts
    samples = total // lines
    specs = [
        pl.BlockSpec((samples, lines, LANES), lambda p: (start + p, 0, 0)),
        pl.BlockSpec((samples, lines, LANES), lambda p: (start + p, 0, 0)),
        pl.BlockSpec(retain.shape, lambda p: (0, 0)),
        pl.BlockSpec((16, LANES), lambda p: (0, 0)),
    ]
    if coded:
        end = prompts * total // 16
        lead = [
            pl.BlockSpec((total, LANES), lambda p: (p, 0)),
            pl.BlockSpec((16, LANES), lambda p: (end, 0)),
        ]
        given = [products, products]
        scratch = [pltpu.VMEM((total, LANES), jnp.float32)]
    else:
        lead = [pl.BlockSpec((1, total, LANES), lambda p: (p, 0, 0))]
        given = [products]
        scratch = []
    return pl.pallas_call(
        functools.partial(combine_kernel, coded, first),
        grid=(prompts,),
        in_specs=lead + specs,
        out_specs=[
            pl.BlockSpec((samples, lines, LANES), lambda p: (p, 0, 0)),
            pl.BlockSpec((16, LANES), lambda p: (0, 0)),
        ],
        out_shape=[
            jax.ShapeDtypeStruct((prompts * samples, lines, LANES), jnp.float32),
            jax.ShapeDtypeStruct((16, LANES), jnp.float32),
        ],
        scratch_shapes=scratch,
        compiler_params=params(16),
        cost_estimate=cost(0, prompts * samples * lines * LANES * 14),
        name="combine",
    )(*given, own, gate, retain, sums)


def finish_kernel(features, first, splits, count, aliased, order_ref, *refs):
    tiles, refs = refs[:count], refs[count:]
    parts, refs = refs[: len(splits)], refs[len(splits) :]
    if aliased:
        refs = refs[1:]
    out_hbm, scratch, scale, sem = refs
    lines = parts[0].shape[1]
    half = lines // 2
    total = sum(t[...] for t in tiles)
    scale[...] = lax.rsqrt(total / features + 1e-05)
    lane = iota((8, LANES), 1)
    at = 0
    for part, count in zip(parts, splits):

        def body(i, carry, part=part, at=at):
            row = at + i
            for j in range(2):
                one = jnp.where(lane == row, scale[j * 8 : j * 8 + 8, :], 0.0)
                one = jnp.sum(one, axis=1, keepdims=True)
                block = part[i, j * half : (j + 1) * half, :].reshape(half // 8, 8, LANES)
                scratch[row, j * half : (j + 1) * half, :] = (block * one[None]).reshape(half, LANES)
            s = order_ref[0, first + row]
            pltpu.make_async_copy(scratch.at[row], out_hbm.at[s], sem).start()
            return carry

        lax.fori_loop(0, count, body, 0, unroll=2)
        at += count
    rows = scratch.shape[0]
    pltpu.make_async_copy(scratch, out_hbm.at[pl.ds(0, rows)], sem).wait()


def finish(order, tiles, parts, first, out, rows):
    splits = tuple(p.shape[0] for p in parts)
    lines = parts[0].shape[1]
    given = [order, *tiles, *parts] + ([out] if out is not None else [])
    specs = [SMEM] + [VMEM] * (len(tiles) + len(parts)) + ([ANY] if out is not None else [])
    count = sum(splits)
    return pl.pallas_call(
        functools.partial(finish_kernel, HEADS * HEAD_DIM, first, splits, len(tiles), out is not None),
        in_specs=specs,
        out_specs=ANY,
        out_shape=jax.ShapeDtypeStruct((rows, lines, LANES), jnp.float32),
        scratch_shapes=[
            pltpu.VMEM((count, lines, LANES), jnp.float32),
            pltpu.VMEM((16, LANES), jnp.float32),
            pltpu.SemaphoreType.DMA,
        ],
        input_output_aliases={len(given) - 1: 0} if out is not None else {},
        compiler_params=params(16),
        cost_estimate=cost(0, count * lines * LANES * 8),
        name="finish",
    )(*given)


def local(
    prefill_states, prompt_slot, sample_prompt, queries, keys, values, gates, norm_gain, decay_rate
):
    group = lax.axis_index("dp")
    groups = lax.axis_size("dp")
    split = lax.axis_size("tensor")
    quarter = groups // 4
    owned = prefill_states.shape[0]
    rows, steps, layers, columns = queries.shape
    heads = columns // LANES
    per = rows // (4 * owned)
    lines = steps * layers * heads
    assert steps == 2 and layers == 2 and per * steps == 8 and rows <= LANES
    assert heads % 4 == 0 and heads * layers * owned <= 2 * LANES

    def swap(block, bits):
        far = [((i // quarter) ^ bits) * quarter + i % quarter for i in range(groups)]
        return lax.ppermute(block, "dp", [(f, i) for i, f in enumerate(far)])

    def shared(tile):
        if split > 4:
            return [lax.psum(tile, "tensor")]
        return [tile] + [
            lax.ppermute(tile, "tensor", [(i, (i + k) % split) for i in range(split)])
            for k in range(1, split)
        ]

    q, k, v, g = (rows_view(x) for x in (queries, keys, values, gates))
    gain = rows_view(norm_gain[None, None]).reshape(heads * layers, LANES)
    retain = jnp.exp(-decay_rate).T.reshape(heads * layers, 1)
    retain = jnp.broadcast_to(retain, (heads * layers, LANES))
    place = (group // quarter).astype(jnp.int32).reshape(1, 1)

    packed = jax.ShapeDtypeStruct((owned, per * lines, LANES), jnp.bfloat16)
    pack_scratch = pltpu.VMEM((2, per * lines, LANES), jnp.float32)
    order, near, next_ = pl.pallas_call(
        functools.partial(order_kernel, owned, quarter, (1, 2)),
        in_specs=[SMEM, VMEM, VMEM, ANY],
        out_specs=[SMEM, VMEM, VMEM],
        out_shape=[jax.ShapeDtypeStruct((1, rows), jnp.int32), packed, packed],
        scratch_shapes=[
            pltpu.VMEM(q.shape, q.dtype),
            pltpu.VMEM((1, rows), jnp.int32),
            pack_scratch,
            pltpu.SemaphoreType.DMA((2,)),
        ],
        compiler_params=params(16),
        cost_estimate=cost(0, 4 << 20),
        name="order",
    )(place, prompt_slot.reshape(1, -1), sample_prompt.reshape(1, -1), q)
    near, next_ = swap(near, 1), swap(next_, 2)
    far, mine = pl.pallas_call(
        functools.partial(pack_kernel, owned, per, (3, 0)),
        in_specs=[SMEM, VMEM],
        out_specs=[VMEM, VMEM],
        out_shape=[packed, packed],
        scratch_shapes=[pack_scratch],
        compiler_params=params(16),
        cost_estimate=cost(0, 4 << 20),
        name="pack",
    )(order, q)
    order, far, mine = lax.optimization_barrier((order, far, mine))
    far = swap(far, 3)

    block = rows // 8
    whole = pl.BlockSpec(q.shape, lambda i: (0, 0, 0))
    flat = pl.BlockSpec(retain.shape, lambda i: (0, 0))
    piece = pl.BlockSpec((block, lines, LANES), lambda i: (i, 0, 0))
    own, gate = pl.pallas_call(
        functools.partial(prepare_kernel, block),
        grid=(rows // block,),
        in_specs=[SMEM] + [whole] * 4 + [flat] * 2,
        out_specs=[piece, piece],
        out_shape=[jax.ShapeDtypeStruct(q.shape, jnp.float32)] * 2,
        compiler_params=params(32),
        cost_estimate=cost(0, 16 << 20),
        name="prepare",
    )(order, q, k, v, g, retain, gain)

    def after(value, *done):
        return lax.optimization_barrier((value, *done))[0]

    zero = jnp.zeros((16, LANES), jnp.float32)
    mine = reach(mine, prefill_states, 0, owned, False)
    near_code = reach(after(near, mine, own), prefill_states, 0, owned, True)
    near = swap(near_code, 1)
    next_code = reach(after(next_, near_code), prefill_states, 0, owned, True)
    next_ = swap(next_code, 2)
    part = owned // 2
    far = after(far, next_code)
    low_code = reach(far, prefill_states, 0, part, True)
    far_low = swap(low_code, 3)
    high_code = reach(after(far, low_code), prefill_states, part, part, True)
    far_high = swap(high_code, 3)

    chunk = owned * per
    out0, sums = combine(False, after(mine, high_code), own, gate, retain, zero, 0, owned, 0)
    out1, sums = combine(True, near, own, gate, retain, sums, owned, owned, chunk)
    out2, sums = combine(True, next_, own, gate, retain, sums, 2 * owned, owned, 2 * chunk)
    early = shared(sums)
    out = finish(order, early, [out0, out1, out2], 0, None, rows)
    out3, sums = combine(True, after(far_low, out), own, gate, retain, zero, 3 * owned, part, 0)
    out4, sums = combine(True, far_high, own, gate, retain, sums, 3 * owned + part, part, part * per)
    late = shared(sums)
    out = finish(order, late, [out3, out4], 3 * chunk, out, rows)
    return rows_unview(out, steps, layers)


def solution(mesh):
    return jax.shard_map(
        local,
        mesh=mesh,
        in_specs=(
            P("dp", None, "tensor", None, None),
            P(),
            P("dp"),
            P("dp", None, None, "tensor"),
            P("dp", None, None, "tensor"),
            P("dp", None, None, "tensor"),
            P("dp", None, None, "tensor"),
            P(None, "tensor"),
            P(None, "tensor"),
        ),
        out_specs=P("dp", None, None, "tensor"),
        check_vma=False,
    )
```

time: 153 us -> 95.2 us (0.62)
  Pallas kernels: 0 us -> 44 us
  local copies, waits for them, and re-layouts: 43.3 us -> 11.4 us
  other arithmetic: 29.5 us -> 0.01 us
  matrix products: 22.7 us -> 0 us
  waiting for transfers between devices: 37 us -> 20 us
  blocking collectives: 11.9 us -> 0 us
  starting transfers between devices: 7.98 us -> 19.1 us
    pallas_call x0 -> x15, Pallas kernels: none -> 44 us  [the longest x5 15.7 us: reach(): pl.pallas_call(functools.partial(reach_kernel, coded), grid=(prompts,), i...]
    dot_general x4 -> x0, matrix products: 22.7 us -> none  [against(): jnp.einsum('psjlhd,plhde->psjlhe', query_block, states, preferred_element...]
    ppermute x6 -> x13, waiting for transfers between devices: 37 us -> 20 us  [the longest x7 12 us: swap(): return lax.ppermute(block, 'dp', [(f, i) for i, f in enumerate(far)])]
    gather x2 -> x0, local copies, waits for them, and re-layouts: 14.1 us -> none  [the longest x1 9.19 us: local(): queries[order]]
    psum x1 -> x0, blocking collectives: 11.9 us -> none  [local(): total = lax.psum(jnp.sum(mixed * mixed, axis=-1), 'tensor')]
    ppermute x6 -> x13, starting transfers between devices: 7.98 us -> 19.1 us  [the longest x7 11.2 us: swap(): return lax.ppermute(block, 'dp', [(f, i) for i, f in enumerate(far)])]
    unnamed x13 -> x26, local copies, waits for them, and re-layouts: 0.03 us -> 11.1 us
    reshape x3 -> x0, local copies, waits for them, and re-layouts: 10.3 us -> none  [the longest x1 4.53 us: local(): key_all = keys.reshape(shape)]
  transfers between devices with their start and end apart: 6 -> 13, of which waited for: 3 -> 7; matrix products, arithmetic and copies ran while one was open for 29% -> 0% of each run, Pallas kernels for 0% -> 40%
where the time goes in v1:
time: 95.2 us; the launch traced here: 94.6 us
  Pallas kernels  44 us (46%)
  waiting for transfers between devices  20 us (21%)
  starting transfers between devices  19.1 us (20%)
  local copies, waits for them, and re-layouts  11.4 us (12%)
    pallas_call x5, Pallas kernels, reach(): pl.pallas_call(functools.partial(reach_kernel, coded), grid=(prompts,), i...  15.7 us
    ppermute x7, waiting for transfers between devices, swap(): return lax.ppermute(block, 'dp', [(f, i) for i, f in enumerate(far)])  12 us
    ppermute x7, starting transfers between devices, swap(): return lax.ppermute(block, 'dp', [(f, i) for i, f in enumerate(far)])  11.2 us
    unnamed x26, local copies, waits for them, and re-layouts  11.1 us
    pallas_call x5, Pallas kernels, combine(): pl.pallas_call(functools.partial(combine_kernel, coded, first), grid=(pro...  8.69 us
    ppermute x6, waiting for transfers between devices, shared(): lax.ppermute(tile, 'tensor', [(i, (i + k) % split) for i in range(split)])  7.94 us
    ppermute x6, starting transfers between devices, shared(): lax.ppermute(tile, 'tensor', [(i, (i + k) % split) for i in range(split)])  7.87 us
    pallas_call x2, Pallas kernels, finish(): pl.pallas_call(functools.partial(finish_kernel, HEADS * HEAD_DIM, first,...  7.82 us
  transfers between devices with their start and end apart: 13, of which 7 were waited for; matrix products, arithmetic and copies ran while one was open for 0% of the time, Pallas kernels for 40%

profile of v1, /device:TPU:0, one launch (start us, length us, event | category | flops | bytes accessed | tf_op | source)
XLA Modules:
  0.0 94.6 jit_solution(4842592143627665751)
XLA Ops:
  0.0 0.0 copy-start.12
  0.0 0.0 copy-start.9
  0.0 1.6 %copy-done.1 = bf16[128,2,2,2048]{3,2,1,0:T(2,128)(2,1)S(1)} copy-done((bf16[128,2,2,2048]{3,2,1,0:T(2,128)(2,1)S(1)}, bf16[128,2,2,2048]{3,2,1,0:T(2,128)(2,1)}, u32[]{:S(2)}) %copy-start.1) | copy-done | bytes 2097176
  1.6 0.0 copy-start.10
  1.6 0.7 copy-done.10
  2.3 0.0 copy-start.11
  2.3 0.7 copy-done.11
  2.9 0.0 copy-start.3
  2.9 2.5 %order.1 = (s32[1,128]{1,0:T(1,128)S(1)}, bf16[8,256,128]{2,1,0:T(8,128)(2,1)}, bf16[8,256,128]{2,1,0:T(8,128)(2,1)}) custom-call(s32[1,1]{1,0:T(1,128)} %bitcast.place_ref, s32[1,64]{1,0:T(1,128)S(1)} %bitcast.42, s32[1,128]{1,0:T(1,128)S(1)} %bitcast.43, bf16[128,64,128]{2,1,0:T(8,128)(2,1)S(1)} %bitcast.35), custom_call_target="tpu_custom_call" | custom-call | bytes 4194304 | tf_op jit(solution)/shard_map/order/pallas_call | solution.py:386
  5.4 3.0 %collective-permute-start.2 = (bf16[8,256,128]{2,1,0:T(8,128)(2,1)}, bf16[8,256,128]{2,1,0:T(8,128)(2,1)}, u32[]{:S(2)}, u32[]{:S(2)}) collective-permute-start(bf16[8,256,128]{2,1,0:T(8,128)(2,1)} %get-tuple-element.37), channel_id=1, source_target_pairs={{8,0},{12,4},{0,8},{4,12},{24,16},{28,20},{16,24},{20,28},{9,1},{1... | collective-permute-start | bytes 1572872 | tf_op jit(solution)/shard_map/ppermute | solution.py:368
  8.4 1.5 %collective-permute-start.1 = (bf16[8,256,128]{2,1,0:T(8,128)(2,1)}, bf16[8,256,128]{2,1,0:T(8,128)(2,1)S(1)}, u32[]{:S(2)}, u32[]{:S(2)}) collective-permute-start(bf16[8,256,128]{2,1,0:T(8,128)(2,1)} %get-tuple-element.36), channel_id=1, source_target_pairs={{16,0},{20,4},{24,8},{28,12},{0,16},{4,20},{8,24},{12,28},{17,1},{... | collective-permute-start | bytes 1572872 | tf_op jit(solution)/shard_map/ppermute | solution.py:368
  10.0 0.0 copy-start.2
  10.0 1.6 %copy-done.2 = bf16[128,2,2,2048]{3,2,1,0:T(2,128)(2,1)S(1)} copy-done((bf16[128,2,2,2048]{3,2,1,0:T(2,128)(2,1)S(1)}, bf16[128,2,2,2048]{3,2,1,0:T(2,128)(2,1)}, u32[]{:S(2)}) %copy-start.2) | copy-done | bytes 2097176
  11.6 1.9 %pack.1 = (bf16[8,256,128]{2,1,0:T(8,128)(2,1)}, bf16[8,256,128]{2,1,0:T(8,128)(2,1)S(1)}) custom-call(s32[1,128]{1,0:T(1,128)S(1)} %get-tuple-element.34.order_ref, bf16[128,64,128]{2,1,0:T(8,128)(2,1)S(1)} %bitcast.36), custom_call_target="tpu_custom_call" | custom-call | bytes 4194304 | tf_op jit(solution)/shard_map/pack/pallas_call | solution.py:402
  13.5 0.8 copy-done.7
  14.2 0.0 collective-permute-start
  14.3 0.0 copy-done.12
  14.3 0.1 copy.22
  14.4 0.1 broadcast_in_dim.10
  14.5 0.1 broadcast_in_dim.11.retain_ref.refs_3_.refs_4_
  14.5 0.0 copy-done.9
  14.5 0.0 copy-done.3
  14.5 1.6 %copy-done.4 = bf16[128,2,2,2048]{3,2,1,0:T(2,128)(2,1)S(1)} copy-done((bf16[128,2,2,2048]{3,2,1,0:T(2,128)(2,1)S(1)}, bf16[128,2,2,2048]{3,2,1,0:T(2,128)(2,1)}, u32[]{:S(2)}) %copy-start.4) | copy-done | bytes 2097176
  16.1 1.6 %copy-done.5 = bf16[128,2,2,2048]{3,2,1,0:T(2,128)(2,1)S(1)} copy-done((bf16[128,2,2,2048]{3,2,1,0:T(2,128)(2,1)S(1)}, bf16[128,2,2,2048]{3,2,1,0:T(2,128)(2,1)}, u32[]{:S(2)}) %copy-start.5) | copy-done | bytes 2097176
  17.7 1.6 %copy-done.6 = bf16[128,2,2,2048]{3,2,1,0:T(2,128)(2,1)S(1)} copy-done((bf16[128,2,2,2048]{3,2,1,0:T(2,128)(2,1)S(1)}, bf16[128,2,2,2048]{3,2,1,0:T(2,128)(2,1)}, u32[]{:S(2)}) %copy-start.6) | copy-done | bytes 2097176
  19.3 7.5 %prepare.1 = (f32[128,64,128]{2,1,0:T(8,128)S(1)}, f32[128,64,128]{2,1,0:T(8,128)S(1)}) custom-call(s32[1,128]{1,0:T(1,128)S(1)} %get-tuple-element.34.order_ref, bf16[128,64,128]{2,1,0:T(8,128)(2,1)S(1)} %bitcast.37, bf16[128,64,128]{2,1,0:T(8,128)(2,1)S(1)} %bitcast.38, bf16[128,64,128]{2,1,0:T(8,128)(2,1)S(1)} %bitcast.39, ...), custom_call_target="tpu_custom_call" | custom-call | bytes 16777216 | tf_op jit(solution)/shard_map/prepare/pallas_call | solution.py:419
  26.8 0.0 copy-done
  26.8 0.0 copy-start.8
  26.8 1.0 %copy-done.8 = bf16[8,256,128]{2,1,0:T(8,128)(2,1)S(1)} copy-done((bf16[8,256,128]{2,1,0:T(8,128)(2,1)S(1)}, bf16[8,256,128]{2,1,0:T(8,128)(2,1)}, u32[]{:S(2)}) %copy-start.8) | copy-done | bytes 524312
  27.9 2.1 %reach.5.refs_0_ = f32[8,256,128]{2,1,0:T(8,128)S(1)} custom-call(bf16[8,256,128]{2,1,0:T(8,128)(2,1)S(1)} %copy-done.8, bf16[8,2,16,128,128]{4,3,2,1,0:T(8,128)(2,1)S(1)} %copy-done), custom_call_target="tpu_custom_call" | custom-call | flops 134217728 | bytes 8388608 | tf_op jit(solution)/shard_map/reach/pallas_call | solution.py:164
  29.9 0.0 collective-permute-done.2.q_ref
  29.9 5.8 %reach.6 = s16[2064,128]{1,0:T(8,128)(2,1)S(1)} custom-call(bf16[8,256,128]{2,1,0:T(8,128)(2,1)} %collective-permute-done.2.q_ref, bf16[8,2,16,128,128]{4,3,2,1,0:T(8,128)(2,1)S(1)} %copy-done), custom_call_target="tpu_custom_call" | custom-call | flops 134217728 | bytes 8388608 | tf_op jit(solution)/shard_map/reach/pallas_call | solution.py:164
  35.7 2.0 %collective-permute-start.6 = (s16[2064,128]{1,0:T(8,128)(2,1)S(1)}, s16[2064,128]{1,0:T(8,128)(2,1)S(1)}, u32[]{:S(2)}, u32[]{:S(2)}) collective-permute-start(s16[2064,128]{1,0:T(8,128)(2,1)S(1)} %reach.6), channel_id=1, source_target_pairs={{8,0},{12,4},{0,8},{4,12},{24,16},{28,20},{16,24},{20,28},{9,1},{1... | collective-permute-start | bytes 1585160 | tf_op jit(solution)/shard_map/ppermute | solution.py:368
  37.8 0.0 collective-permute-done.1.q_ref
  37.8 3.9 %reach.7 = s16[2064,128]{1,0:T(8,128)(2,1)S(1)} custom-call(bf16[8,256,128]{2,1,0:T(8,128)(2,1)S(1)} %collective-permute-done.1.q_ref, bf16[8,2,16,128,128]{4,3,2,1,0:T(8,128)(2,1)S(1)} %copy-done), custom_call_target="tpu_custom_call" | custom-call | flops 134217728 | bytes 8388608 | tf_op jit(solution)/shard_map/reach/pallas_call | solution.py:164
  41.7 1.6 %collective-permute-start.5 = (s16[2064,128]{1,0:T(8,128)(2,1)S(1)}, s16[2064,128]{1,0:T(8,128)(2,1)S(1)}, u32[]{:S(2)}, u32[]{:S(2)}) collective-permute-start(s16[2064,128]{1,0:T(8,128)(2,1)S(1)} %reach.7), channel_id=1, source_target_pairs={{16,0},{20,4},{24,8},{28,12},{0,16},{4,20},{8,24},{12,28},{17,1},{... | collective-permute-start | bytes 1585160 | tf_op jit(solution)/shard_map/ppermute | solution.py:368
  43.2 0.0 collective-permute-done.q_ref
  43.2 1.9 %reach.8 = s16[1040,128]{1,0:T(8,128)(2,1)S(1)} custom-call(bf16[8,256,128]{2,1,0:T(8,128)(2,1)S(1)} %collective-permute-done.q_ref, bf16[8,2,16,128,128]{4,3,2,1,0:T(8,128)(2,1)S(1)} %copy-done), custom_call_target="tpu_custom_call" | custom-call | flops 67108864 | bytes 4194304 | tf_op jit(solution)/shard_map/reach/pallas_call | solution.py:164
  45.2 0.1 collective-permute-start.4
  45.3 2.0 %reach.9 = s16[1040,128]{1,0:T(8,128)(2,1)S(1)} custom-call(bf16[8,256,128]{2,1,0:T(8,128)(2,1)S(1)} %collective-permute-done.q_ref, bf16[8,2,16,128,128]{4,3,2,1,0:T(8,128)(2,1)S(1)} %copy-done), custom_call_target="tpu_custom_call" | custom-call | flops 67108864 | bytes 4194304 | tf_op jit(solution)/shard_map/reach/pallas_call | solution.py:164
  47.2 3.0 %collective-permute-start.3 = (s16[1040,128]{1,0:T(8,128)(2,1)S(1)}, s16[1040,128]{1,0:T(8,128)(2,1)S(1)}, u32[]{:S(2)}, u32[]{:S(2)}) collective-permute-start(s16[1040,128]{1,0:T(8,128)(2,1)S(1)} %reach.9), channel_id=1, source_target_pairs={{24,0},{28,4},{16,8},{20,12},{8,16},{12,20},{0,24},{4,28},{25,1},{... | collective-permute-start | bytes 798728 | tf_op jit(solution)/shard_map/ppermute | solution.py:368
  50.2 0.9 combine.5
  51.2 0.0 collective-permute-done.6.refs_0_.refs_1_
  51.2 2.6 %combine.6 = (f32[32,64,128]{2,1,0:T(8,128)S(1)}, f32[16,128]{1,0:T(8,128)S(1)}) custom-call(s16[2064,128]{1,0:T(8,128)(2,1)S(1)} %collective-permute-done.6.refs_0_.refs_1_, s16[2064,128]{1,0:T(8,128)(2,1)S(1)} %collective-permute-done.6.refs_0_.refs_1_, f32[128,64,128]{2,1,0:T(8,128)S(1)} %get-tuple-element.39.refs_1_.refs_2_, ...), custom_call_target="tpu_custom_call" | custom-call | bytes 3670016 | tf_op jit(solution)/shard_map/combine/pallas_call | solution.py:278
  53.8 12.0 %collective-permute-done.5.refs_0_.refs_1_ = s16[2064,128]{1,0:T(8,128)(2,1)S(1)} collective-permute-done((s16[2064,128]{1,0:T(8,128)(2,1)S(1)}, s16[2064,128]{1,0:T(8,128)(2,1)S(1)}, u32[]{:S(2)}, u32[]{:S(2)}) %collective-permute-start.5) | collective-permute-done | bytes 528416 | tf_op jit(solution)/shard_map/ppermute | solution.py:368
  65.8 2.6 %combine.7 = (f32[32,64,128]{2,1,0:T(8,128)S(1)}, f32[16,128]{1,0:T(8,128)S(1)}) custom-call(s16[2064,128]{1,0:T(8,128)(2,1)S(1)} %collective-permute-done.5.refs_0_.refs_1_, s16[2064,128]{1,0:T(8,128)(2,1)S(1)} %collective-permute-done.5.refs_0_.refs_1_, f32[128,64,128]{2,1,0:T(8,128)S(1)} %get-tuple-element.39.refs_1_.refs_2_, ...), custom_call_target="tpu_custom_call" | custom-call | bytes 3670016 | tf_op jit(solution)/shard_map/combine/pallas_call | solution.py:278
  68.3 3.7 %collective-permute-start.9 = (f32[16,128]{1,0:T(8,128)S(1)}, f32[16,128]{1,0:T(8,128)S(1)}, u32[]{:S(2)}, u32[]{:S(2)}) collective-permute-start(f32[16,128]{1,0:T(8,128)S(1)} %get-tuple-element.48.refs_0_), channel_id=1, source_target_pairs={{0,3},{1,0},{2,1},{3,2},{4,7},{5,4},{6,5},{7,6},{8,11},{9,8},{10,9... | collective-permute-start | bytes 24584 | tf_op jit(solution)/shard_map/ppermute | solution.py:374
  72.0 0.0 collective-permute-start.8
  72.0 1.0 %collective-permute-start.7 = (f32[16,128]{1,0:T(8,128)S(1)}, f32[16,128]{1,0:T(8,128)S(1)}, u32[]{:S(2)}, u32[]{:S(2)}) collective-permute-start(f32[16,128]{1,0:T(8,128)S(1)} %get-tuple-element.48.refs_0_), channel_id=1, source_target_pairs={{0,1},{1,2},{2,3},{3,0},{4,5},{5,6},{6,7},{7,4},{8,9},{9,10},{10,1... | collective-permute-start | bytes 24584 | tf_op jit(solution)/shard_map/ppermute | solution.py:374
  73.0 0.4 collective-permute-done.9.refs_3_
  73.4 3.2 %collective-permute-done.8.refs_2_ = f32[16,128]{1,0:T(8,128)S(1)} collective-permute-done((f32[16,128]{1,0:T(8,128)S(1)}, f32[16,128]{1,0:T(8,128)S(1)}, u32[]{:S(2)}, u32[]{:S(2)}) %collective-permute-start.8) | collective-permute-done | bytes 8224 | tf_op jit(solution)/shard_map/ppermute | solution.py:374
  76.5 0.9 collective-permute-done.7.refs_1_
  77.4 5.3 %finish.2.refs_6_ = f32[128,64,128]{2,1,0:T(8,128)} custom-call(s32[1,128]{1,0:T(1,128)S(1)} %get-tuple-element.34.order_ref, f32[16,128]{1,0:T(8,128)S(1)} %get-tuple-element.48.refs_0_, f32[16,128]{1,0:T(8,128)S(1)} %collective-permute-done.7.refs_1_, f32[16,128]{1,0:T(8,128)S(1)} %collective-permute-done.8.refs_2_, ...), custom_call_target="tpu_custom_call" | custom-call | bytes 6291456 | tf_op jit(solution)/shard_map/finish/pallas_call | solution.py:334
  82.7 0.0 collective-permute-done.4.refs_0_.refs_1_
  82.7 1.3 %combine.8 = (f32[16,64,128]{2,1,0:T(8,128)S(1)}, f32[16,128]{1,0:T(8,128)S(1)}) custom-call(s16[1040,128]{1,0:T(8,128)(2,1)S(1)} %collective-permute-done.4.refs_0_.refs_1_, s16[1040,128]{1,0:T(8,128)(2,1)S(1)} %collective-permute-done.4.refs_0_.refs_1_, f32[128,64,128]{2,1,0:T(8,128)S(1)} %get-tuple-element.39.refs_1_.refs_2_, ...), custom_call_target="tpu_custom_call" | custom-call | bytes 1835008 | tf_op jit(solution)/shard_map/combine/pallas_call | solution.py:278
  84.0 0.0 collective-permute-done.3.refs_0_.refs_1_
  84.0 1.3 %combine.9 = (f32[16,64,128]{2,1,0:T(8,128)S(1)}, f32[16,128]{1,0:T(8,128)S(1)}) custom-call(s16[1040,128]{1,0:T(8,128)(2,1)S(1)} %collective-permute-done.3.refs_0_.refs_1_, s16[1040,128]{1,0:T(8,128)(2,1)S(1)} %collective-permute-done.3.refs_0_.refs_1_, f32[128,64,128]{2,1,0:T(8,128)S(1)} %get-tuple-element.39.refs_1_.refs_2_, ...), custom_call_target="tpu_custom_call" | custom-call | bytes 1835008 | tf_op jit(solution)/shard_map/combine/pallas_call | solution.py:278
  85.4 0.6 collective-permute-start.12
  86.0 0.6 collective-permute-start.11
  86.6 1.9 %collective-permute-start.10 = (f32[16,128]{1,0:T(8,128)S(1)}, f32[16,128]{1,0:T(8,128)S(1)}, u32[]{:S(2)}, u32[]{:S(2)}) collective-permute-start(f32[16,128]{1,0:T(8,128)S(1)} %get-tuple-element.54.refs_0_), channel_id=1, source_target_pairs={{0,1},{1,2},{2,3},{3,0},{4,5},{5,6},{6,7},{7,4},{8,9},{9,10},{10,1... | collective-permute-start | bytes 24584 | tf_op jit(solution)/shard_map/ppermute | solution.py:374
  88.6 0.5 collective-permute-done.12.refs_3_
  89.1 1.5 %collective-permute-done.11.refs_2_ = f32[16,128]{1,0:T(8,128)S(1)} collective-permute-done((f32[16,128]{1,0:T(8,128)S(1)}, f32[16,128]{1,0:T(8,128)S(1)}, u32[]{:S(2)}, u32[]{:S(2)}) %collective-permute-start.11) | collective-permute-done | bytes 8224 | tf_op jit(solution)/shard_map/ppermute | solution.py:374
  90.5 1.5 %collective-permute-done.10.refs_1_ = f32[16,128]{1,0:T(8,128)S(1)} collective-permute-done((f32[16,128]{1,0:T(8,128)S(1)}, f32[16,128]{1,0:T(8,128)S(1)}, u32[]{:S(2)}, u32[]{:S(2)}) %collective-permute-start.10) | collective-permute-done | bytes 8224 | tf_op jit(solution)/shard_map/ppermute | solution.py:374
  92.1 2.6 %finish.3 = f32[128,64,128]{2,1,0:T(8,128)} custom-call(s32[1,128]{1,0:T(1,128)S(1)} %get-tuple-element.34.order_ref, f32[16,128]{1,0:T(8,128)S(1)} %get-tuple-element.54.refs_0_, f32[16,128]{1,0:T(8,128)S(1)} %collective-permute-done.10.refs_1_, f32[16,128]{1,0:T(8,128)S(1)} %collective-permute-done.11.refs_2_, ...), custom_call_target="tpu_custom_call", output_to_operand_aliasing={{}: (7, {})} | custom-call | bytes 2097152 | tf_op jit(solution)/shard_map/finish/pallas_call | solution.py:334
  (8 shorter events, 0.0 us)
Async XLA Ops:
  0.0 14.3 %copy-start.12 = (f32[2,16]{1,0:T(2,128)S(1)}, f32[2,16]{1,0:T(2,128)}, u32[]{:S(2)}) copy-start(f32[2,16]{1,0:T(2,128)} %param.17) | copy-start | bytes 388
  0.0 14.5 %copy-start.9 = (f32[2,2048]{1,0:T(2,128)S(1)}, f32[2,2048]{1,0:T(2,128)}, u32[]{:S(2)}) copy-start(f32[2,2048]{1,0:T(2,128)} %param.16) | copy-start | bytes 49156
  0.0 1.6 %copy-start.1 = (bf16[128,2,2,2048]{3,2,1,0:T(2,128)(2,1)S(1)}, bf16[128,2,2,2048]{3,2,1,0:T(2,128)(2,1)}, u32[]{:S(2)}) copy-start(bf16[128,2,2,2048]{3,2,1,0:T(2,128)(2,1)} %param.12) | copy-start | bytes 6291460
  1.6 0.7 copy-start.10
  2.3 0.7 copy-start.11
  2.9 11.6 %copy-start.3 = (bf16[128,2,2,2048]{3,2,1,0:T(2,128)(2,1)S(1)}, bf16[128,2,2,2048]{3,2,1,0:T(2,128)(2,1)}, u32[]{:S(2)}) copy-start(bf16[128,2,2,2048]{3,2,1,0:T(2,128)(2,1)} %param.12) | copy-start | bytes 6291460
  5.4 24.5 %collective-permute-start.2 = (bf16[8,256,128]{2,1,0:T(8,128)(2,1)}, bf16[8,256,128]{2,1,0:T(8,128)(2,1)}, u32[]{:S(2)}, u32[]{:S(2)}) collective-permute-start(bf16[8,256,128]{2,1,0:T(8,128)(2,1)} %get-tuple-element.37), channel_id=1, source_target_pairs={{8,0},{12,4},{0,8},{4,12},{24,16},{28,20},{16,24},{20,28},{9,1},{1... | collective-permute-start | bytes 1572872 | tf_op jit(solution)/shard_map/ppermute | solution.py:368
  8.4 29.3 %collective-permute-start.1 = (bf16[8,256,128]{2,1,0:T(8,128)(2,1)}, bf16[8,256,128]{2,1,0:T(8,128)(2,1)S(1)}, u32[]{:S(2)}, u32[]{:S(2)}) collective-permute-start(bf16[8,256,128]{2,1,0:T(8,128)(2,1)} %get-tuple-element.36), channel_id=1, source_target_pairs={{16,0},{20,4},{24,8},{28,12},{0,16},{4,20},{8,24},{12,28},{17,1},{... | collective-permute-start | bytes 1572872 | tf_op jit(solution)/shard_map/ppermute | solution.py:368
  10.0 1.6 %copy-start.2 = (bf16[128,2,2,2048]{3,2,1,0:T(2,128)(2,1)S(1)}, bf16[128,2,2,2048]{3,2,1,0:T(2,128)(2,1)}, u32[]{:S(2)}) copy-start(bf16[128,2,2,2048]{3,2,1,0:T(2,128)(2,1)} %param.12) | copy-start | bytes 6291460
  13.5 0.8 copy-start.7
  14.2 29.0 %collective-permute-start = (bf16[8,256,128]{2,1,0:T(8,128)(2,1)}, bf16[8,256,128]{2,1,0:T(8,128)(2,1)S(1)}, u32[]{:S(2)}, u32[]{:S(2)}) collective-permute-start(bf16[8,256,128]{2,1,0:T(8,128)(2,1)} %get-tuple-element.35), channel_id=1, source_target_pairs={{24,0},{28,4},{16,8},{20,12},{8,16},{12,20},{0,24},{4,28},{25,1},{... | collective-permute-start | bytes 1572872 | tf_op jit(solution)/shard_map/ppermute | solution.py:368
  14.5 1.6 %copy-start.4 = (bf16[128,2,2,2048]{3,2,1,0:T(2,128)(2,1)S(1)}, bf16[128,2,2,2048]{3,2,1,0:T(2,128)(2,1)}, u32[]{:S(2)}) copy-start(bf16[128,2,2,2048]{3,2,1,0:T(2,128)(2,1)} %param.13) | copy-start | bytes 6291460
  16.1 1.6 %copy-start.5 = (bf16[128,2,2,2048]{3,2,1,0:T(2,128)(2,1)S(1)}, bf16[128,2,2,2048]{3,2,1,0:T(2,128)(2,1)}, u32[]{:S(2)}) copy-start(bf16[128,2,2,2048]{3,2,1,0:T(2,128)(2,1)} %param.14) | copy-start | bytes 6291460
  17.7 1.6 %copy-start.6 = (bf16[128,2,2,2048]{3,2,1,0:T(2,128)(2,1)S(1)}, bf16[128,2,2,2048]{3,2,1,0:T(2,128)(2,1)}, u32[]{:S(2)}) copy-start(bf16[128,2,2,2048]{3,2,1,0:T(2,128)(2,1)} %param.15) | copy-start | bytes 6291460
  19.3 7.5 %copy-start = (bf16[8,2,16,128,128]{4,3,2,1,0:T(8,128)(2,1)S(1)}, bf16[8,2,16,128,128]{4,3,2,1,0:T(8,128)(2,1)}, u32[]{:S(2)}) copy-start(bf16[8,2,16,128,128]{4,3,2,1,0:T(8,128)(2,1)} %s_ref.9) | copy-start | bytes 25165828
  26.8 1.0 %copy-start.8 = (bf16[8,256,128]{2,1,0:T(8,128)(2,1)S(1)}, bf16[8,256,128]{2,1,0:T(8,128)(2,1)}, u32[]{:S(2)}) copy-start(bf16[8,256,128]{2,1,0:T(8,128)(2,1)} %copy-done.7) | copy-start | bytes 1572868
  35.7 15.4 %collective-permute-start.6 = (s16[2064,128]{1,0:T(8,128)(2,1)S(1)}, s16[2064,128]{1,0:T(8,128)(2,1)S(1)}, u32[]{:S(2)}, u32[]{:S(2)}) collective-permute-start(s16[2064,128]{1,0:T(8,128)(2,1)S(1)} %reach.6), channel_id=1, source_target_pairs={{8,0},{12,4},{0,8},{4,12},{24,16},{28,20},{16,24},{20,28},{9,1},{1... | collective-permute-start | bytes 1585160 | tf_op jit(solution)/shard_map/ppermute | solution.py:368
  41.7 24.1 %collective-permute-start.5 = (s16[2064,128]{1,0:T(8,128)(2,1)S(1)}, s16[2064,128]{1,0:T(8,128)(2,1)S(1)}, u32[]{:S(2)}, u32[]{:S(2)}) collective-permute-start(s16[2064,128]{1,0:T(8,128)(2,1)S(1)} %reach.7), channel_id=1, source_target_pairs={{16,0},{20,4},{24,8},{28,12},{0,16},{4,20},{8,24},{12,28},{17,1},{... | collective-permute-start | bytes 1585160 | tf_op jit(solution)/shard_map/ppermute | solution.py:368
  45.2 37.5 %collective-permute-start.4 = (s16[1040,128]{1,0:T(8,128)(2,1)S(1)}, s16[1040,128]{1,0:T(8,128)(2,1)S(1)}, u32[]{:S(2)}, u32[]{:S(2)}) collective-permute-start(s16[1040,128]{1,0:T(8,128)(2,1)S(1)} %reach.8), channel_id=1, source_target_pairs={{24,0},{28,4},{16,8},{20,12},{8,16},{12,20},{0,24},{4,28},{25,1},{... | collective-permute-start | bytes 798728 | tf_op jit(solution)/shard_map/ppermute | solution.py:368
  47.2 36.8 %collective-permute-start.3 = (s16[1040,128]{1,0:T(8,128)(2,1)S(1)}, s16[1040,128]{1,0:T(8,128)(2,1)S(1)}, u32[]{:S(2)}, u32[]{:S(2)}) collective-permute-start(s16[1040,128]{1,0:T(8,128)(2,1)S(1)} %reach.9), channel_id=1, source_target_pairs={{24,0},{28,4},{16,8},{20,12},{8,16},{12,20},{0,24},{4,28},{25,1},{... | collective-permute-start | bytes 798728 | tf_op jit(solution)/shard_map/ppermute | solution.py:368
  68.3 5.0 %collective-permute-start.9 = (f32[16,128]{1,0:T(8,128)S(1)}, f32[16,128]{1,0:T(8,128)S(1)}, u32[]{:S(2)}, u32[]{:S(2)}) collective-permute-start(f32[16,128]{1,0:T(8,128)S(1)} %get-tuple-element.48.refs_0_), channel_id=1, source_target_pairs={{0,3},{1,0},{2,1},{3,2},{4,7},{5,4},{6,5},{7,6},{8,11},{9,8},{10,9... | collective-permute-start | bytes 24584 | tf_op jit(solution)/shard_map/ppermute | solution.py:374
  72.0 4.5 %collective-permute-start.8 = (f32[16,128]{1,0:T(8,128)S(1)}, f32[16,128]{1,0:T(8,128)S(1)}, u32[]{:S(2)}, u32[]{:S(2)}) collective-permute-start(f32[16,128]{1,0:T(8,128)S(1)} %get-tuple-element.48.refs_0_), channel_id=1, source_target_pairs={{0,2},{1,3},{2,0},{3,1},{4,6},{5,7},{6,4},{7,5},{8,10},{9,11},{10,... | collective-permute-start | bytes 24584 | tf_op jit(solution)/shard_map/ppermute | solution.py:374
  72.0 5.4 %collective-permute-start.7 = (f32[16,128]{1,0:T(8,128)S(1)}, f32[16,128]{1,0:T(8,128)S(1)}, u32[]{:S(2)}, u32[]{:S(2)}) collective-permute-start(f32[16,128]{1,0:T(8,128)S(1)} %get-tuple-element.48.refs_0_), channel_id=1, source_target_pairs={{0,1},{1,2},{2,3},{3,0},{4,5},{5,6},{6,7},{7,4},{8,9},{9,10},{10,1... | collective-permute-start | bytes 24584 | tf_op jit(solution)/shard_map/ppermute | solution.py:374
  85.4 3.7 %collective-permute-start.12 = (f32[16,128]{1,0:T(8,128)S(1)}, f32[16,128]{1,0:T(8,128)S(1)}, u32[]{:S(2)}, u32[]{:S(2)}) collective-permute-start(f32[16,128]{1,0:T(8,128)S(1)} %get-tuple-element.54.refs_0_), channel_id=1, source_target_pairs={{0,3},{1,0},{2,1},{3,2},{4,7},{5,4},{6,5},{7,6},{8,11},{9,8},{10,9... | collective-permute-start | bytes 24584 | tf_op jit(solution)/shard_map/ppermute | solution.py:374
  86.0 4.5 %collective-permute-start.11 = (f32[16,128]{1,0:T(8,128)S(1)}, f32[16,128]{1,0:T(8,128)S(1)}, u32[]{:S(2)}, u32[]{:S(2)}) collective-permute-start(f32[16,128]{1,0:T(8,128)S(1)} %get-tuple-element.54.refs_0_), channel_id=1, source_target_pairs={{0,2},{1,3},{2,0},{3,1},{4,6},{5,7},{6,4},{7,5},{8,10},{9,11},{10,... | collective-permute-start | bytes 24584 | tf_op jit(solution)/shard_map/ppermute | solution.py:374
  86.6 5.4 %collective-permute-start.10 = (f32[16,128]{1,0:T(8,128)S(1)}, f32[16,128]{1,0:T(8,128)S(1)}, u32[]{:S(2)}, u32[]{:S(2)}) collective-permute-start(f32[16,128]{1,0:T(8,128)S(1)} %get-tuple-element.54.refs_0_), channel_id=1, source_target_pairs={{0,1},{1,2},{2,3},{3,0},{4,5},{5,6},{6,7},{7,4},{8,9},{9,10},{10,1... | collective-permute-start | bytes 24584 | tf_op jit(solution)/shard_map/ppermute | solution.py:374

commit v2 on v0

v2 whole, which is shorter than its diff:
```python
import functools

import jax
import jax.numpy as jnp
from jax import lax
from jax.experimental import pallas as pl
from jax.experimental.pallas import tpu as pltpu
from jax.sharding import PartitionSpec as P

HEADS = 64
HEAD_DIM = 128
LANES = 128
ANY = pl.BlockSpec(memory_space=pl.ANY)
SMEM = pl.BlockSpec(memory_space=pltpu.SMEM)
VMEM = pl.BlockSpec(memory_space=pltpu.VMEM)
TOP = 32767.0
ROUND = 12582912.0
BIG = 54
FAR = 2


def params(mib):
    return pltpu.CompilerParams(vmem_limit_bytes=mib << 20)


def cost(flops, moved):
    return pl.CostEstimate(flops=flops, bytes_accessed=moved, transcendentals=0)


def rows_view(x):
    rows, steps, layers, columns = x.shape
    heads = columns // LANES
    x = x.reshape(rows, steps, layers, heads, LANES).transpose(0, 1, 3, 2, 4)
    return x.reshape(rows, steps * heads * layers, LANES)


def rows_unview(y, steps, layers):
    rows, lines, _ = y.shape
    heads = lines // (steps * layers)
    y = y.reshape(rows, steps, heads, layers, LANES).transpose(0, 1, 3, 2, 4)
    return y.reshape(rows, steps, layers, heads * LANES)


def iota(shape, axis):
    return lax.broadcasted_iota(jnp.int32, shape, axis)


def pack_rows(order_ref, first, prompts, q_ref, scratch, out_ref):
    lines = q_ref.shape[1]
    half = lines // 2
    total = out_ref.shape[1]
    samples = total // lines

    def body(p, carry):
        for c in range(samples):
            s = order_ref[0, first + p * samples + c]
            for j in range(2):
                block = q_ref[s, j * half : (j + 1) * half, :].astype(jnp.float32)
                scratch[p % 2, pl.ds(c * 2 + j, half, stride=2 * samples), :] = block
        out_ref[p] = scratch[p % 2].astype(jnp.bfloat16)
        return carry

    lax.fori_loop(0, prompts, body, 0, unroll=2)


def order_kernel(
    owned, quarter, chunks, place_ref, slot_hbm, prompt_hbm, q_hbm,
    order_ref, *rest,
):
    outs = rest[: len(chunks)]
    q_vmem, slot_ref, prompt_ref, line, scratch, sems = rest[len(chunks) :]
    small = [
        pltpu.make_async_copy(slot_hbm, slot_ref, sems.at[2]),
        pltpu.make_async_copy(prompt_hbm, prompt_ref, sems.at[3]),
    ]
    load = pltpu.make_async_copy(q_hbm, q_vmem, sems.at[0])
    for copy in small:
        copy.start()
    load.start()
    for copy in small:
        copy.wait()
    rows = prompt_ref.shape[1]
    count = slot_ref.shape[1]
    per = rows // (4 * owned)
    f32 = jnp.float32
    slot = slot_ref[...]
    owner = lax.div(lax.div(slot, owned), quarter)
    table = ((owner ^ place_ref[0, 0]) * owned + lax.rem(slot, owned)).astype(f32)
    down, across = iota((rows, rows), 0), iota((rows, rows), 1)
    prompt = jnp.broadcast_to(prompt_ref[...].astype(f32), (rows, rows))
    prompt = jnp.sum(jnp.where(down == across, prompt, 0.0), axis=1, keepdims=True)
    hit = prompt == iota((rows, count), 1).astype(f32)
    key = jnp.sum(jnp.where(hit, jnp.broadcast_to(table, (rows, count)), 0.0), axis=1, keepdims=True)
    key_all = jnp.broadcast_to(key, (rows, rows))
    key_row = jnp.sum(jnp.where(down == across, key_all, 0.0), axis=0, keepdims=True)
    same = (key_all == jnp.broadcast_to(key_row, (rows, rows))) & (across < down)
    rank = jnp.sum(jnp.where(same, 1.0, 0.0), axis=1, keepdims=True)
    spot = key * per + rank
    found = jnp.broadcast_to(spot, (rows, rows)) == across.astype(f32)
    line[...] = jnp.sum(jnp.where(found, down.astype(f32), 0.0), axis=0, keepdims=True).astype(jnp.int32)
    note = pltpu.make_async_copy(line, order_ref, sems.at[1])
    note.start()
    note.wait()
    load.wait()
    for chunk, out_ref in zip(chunks, outs):
        pack_rows(order_ref, chunk * owned * per, owned, q_vmem, scratch, out_ref)


def reach_kernel(coded, begin, prompts, q_ref, s_ref, out_ref, *scratch):
    heads = s_ref.shape[2]
    lines = q_ref.shape[1]
    lane = iota((8, LANES), 1)

    def products(p, h):
        a = q_ref[begin + p, h * 16 : (h + 1) * 16, :]
        w = jnp.concatenate([s_ref[begin + p, 0, h], s_ref[begin + p, 1, h]], axis=1)
        y = jnp.dot(a, w, preferred_element_type=jnp.float32)
        return y[:8, :LANES], y[8:, LANES:]

    def plain(p, carry):
        for h in range(heads):
            for l, r in enumerate(products(p, h)):
                at = h * 16 + l * 8
                out_ref[p, at : at + 8, :] = r
        return carry

    def code(t, carry):
        power = scratch[0]
        base = t * 2 * heads
        mine = (lane >= base) & (lane < base + 2 * heads)
        for slot in range(2):
            p = t * 2 + slot
            exponents = jnp.zeros((8, LANES), jnp.float32)
            for h in range(heads):
                pair = []
                for l, r in enumerate(products(p, h)):
                    top = jnp.max(jnp.abs(r), axis=1, keepdims=True)
                    e = jnp.ceil(jnp.log2(jnp.maximum(top, 1e-32)) + 1e-4)
                    exponents = jnp.where(lane == h * 2 + l, e, exponents)
                    pair.append((r * (jnp.exp2(15.0 - e) * (TOP / 32768.0)) + ROUND) - ROUND)
                pair = jnp.concatenate(pair, axis=0).astype(jnp.int32).astype(jnp.int16)
                out_ref[pl.ds(pl.multiple_of(p * lines + h * 16, 16), 16), :] = pair
            at = slice(slot * 8, slot * 8 + 8)
            power[at, :] = jnp.where(mine, pltpu.roll(exponents, base, 1), power[at, :])
        return carry

    if not coded:
        lax.fori_loop(0, prompts, plain, 0)
        return
    scratch[0][...] = jnp.zeros_like(scratch[0])
    lax.fori_loop(0, prompts // 2, code, 0, unroll=2)
    tail = prompts * lines
    out_ref[tail : tail + 16, :] = scratch[0][...].astype(jnp.int32).astype(jnp.int16)


def reach(query, states, begin, prompts, coded):
    _, lines, _ = query.shape
    _, layers, heads, _, _ = states.shape
    if coded:
        shape = jax.ShapeDtypeStruct((prompts * lines + 16, LANES), jnp.int16)
        scratch = [pltpu.VMEM((16, LANES), jnp.float32)]
    else:
        shape = jax.ShapeDtypeStruct((prompts, lines, LANES), jnp.float32)
        scratch = []
    return pl.pallas_call(
        functools.partial(reach_kernel, coded, begin, prompts),
        in_specs=[VMEM, VMEM],
        out_specs=VMEM,
        out_shape=shape,
        scratch_shapes=scratch,
        compiler_params=params(16),
        cost_estimate=cost(prompts * lines * LANES * LANES * 4, prompts * layers * heads * LANES * LANES * 2),
        name="reach",
    )(query, states)


def retained(decay_ref):
    layers, heads = decay_ref.shape
    line, head = iota((layers * heads, heads), 0), iota((layers * heads, heads), 1)
    rate = jnp.broadcast_to(decay_ref[0:1, :], (layers * heads, heads))
    other = jnp.broadcast_to(decay_ref[1:2, :], (layers * heads, heads))
    rate = jnp.where(line % 2 == 0, rate, other)
    rate = jnp.sum(jnp.where(line // 2 == head, rate, 0.0), axis=1, keepdims=True)
    return jnp.broadcast_to(jnp.exp(-rate), (layers * heads, LANES))


def row_terms(q_ref, k_ref, v_ref, g_ref, retain_ref, gain_ref, s):
    half = q_ref.shape[1] // 2
    f32 = jnp.float32
    one, two = slice(0, half), slice(half, 2 * half)
    retain, gain = retain_ref[...], gain_ref[...]
    q1, q2 = q_ref[s, one, :].astype(f32), q_ref[s, two, :].astype(f32)
    k1, k2 = k_ref[s, one, :].astype(f32), k_ref[s, two, :].astype(f32)
    v1, v2 = v_ref[s, one, :].astype(f32), v_ref[s, two, :].astype(f32)
    first_first = jnp.sum(q1 * k1, axis=1, keepdims=True)
    second_first = jnp.sum(q2 * k1, axis=1, keepdims=True)
    second_second = jnp.sum(q2 * k2, axis=1, keepdims=True)
    own = first_first * v1, retain * second_first * v1 + second_second * v2
    return own, [gain * jax.nn.sigmoid(g_ref[s, at, :].astype(f32)) for at in (one, two)]


def pack_kernel(
    per, owned, first, order_ref, decay_ref, gain_ref, q_hbm, k_hbm, v_hbm, g_hbm,
    far_ref, mine_ref, own_hbm, gate_hbm,
    q_ref, k_ref, v_ref, g_ref, own_ref, gate_ref, retain_ref, scratch, sems,
):
    half = q_ref.shape[1] // 2
    pairs = ((q_hbm, q_ref), (k_hbm, k_ref), (v_hbm, v_ref), (g_hbm, g_ref))
    loads = [pltpu.make_async_copy(a, b, sems.at[i]) for i, (a, b) in enumerate(pairs)]
    for copy in loads:
        copy.start()
    retain_ref[...] = retained(decay_ref)
    loads[0].wait()
    pack_rows(order_ref, 3 * owned * per, owned, q_ref, scratch, far_ref)
    pack_rows(order_ref, 0, owned, q_ref, scratch, mine_ref)
    for copy in loads[1:]:
        copy.wait()

    def body(i, carry):
        s = order_ref[0, first + i]
        own, gate = row_terms(q_ref, k_ref, v_ref, g_ref, retain_ref, gain_ref, s)
        for j in range(2):
            at = slice(j * half, (j + 1) * half)
            own_ref[i, at, :] = own[j]
            gate_ref[i, at, :] = gate[j]
        return carry

    rows = own_ref.shape[0]
    stores = []
    for n in range(4):
        at = pl.ds(n * (rows // 4), rows // 4)
        lax.fori_loop(n * (rows // 4), (n + 1) * (rows // 4), body, 0, unroll=2)
        for m, (a, b) in enumerate(((own_ref, own_hbm), (gate_ref, gate_hbm))):
            stores.append(pltpu.make_async_copy(a.at[at], b.at[at], sems.at[4 + 2 * n + m]))
            stores[-1].start()
    for copy in stores:
        copy.wait()


def combine_kernel(parts, inline, order_ref, decay_ref, sum_in, *refs):
    given, refs = refs[: 5 if inline else 2], refs[5 if inline else 2 :]
    product_refs, refs = refs[: len(parts)], refs[len(parts) :]
    out_refs, (sum_ref, retain_ref, unit_ref, exact) = refs[: len(parts)], refs[len(parts) :]
    half, total = retain_ref.shape[0], exact.shape[1]
    lane = iota((8, LANES), 1)
    retain_ref[...] = retained(decay_ref)
    zero = jnp.zeros((8, LANES), jnp.float32)
    totals = (zero, zero)
    for (coded, first, prompts, place), product_ref, out_ref in zip(parts, product_refs, out_refs):
        samples = out_ref.shape[0] // prompts
        if coded:
            power = product_ref[prompts * total : prompts * total + 16, :]
            unit_ref[...] = jnp.exp2(power.astype(jnp.int32).astype(jnp.float32) - 15.0) * (32768.0 / TOP)

        def body(t, totals, coded=coded, first=first, place=place, product_ref=product_ref, out_ref=out_ref, samples=samples):
            totals = list(totals)
            for slot in range(2):
                p = t * 2 + slot
                if coded:
                    unit = unit_ref[slot * 8 : slot * 8 + 8, :]
                    unit = pltpu.roll(unit, lax.rem(LANES - t * half, LANES), 1)
                    for h in range(half // 2):
                        code = product_ref[pl.ds(pl.multiple_of(p * total + h * 16, 16), 16), :]
                        code = code.astype(jnp.int32).astype(jnp.float32)
                        for l in range(2):
                            at = h * 16 + l * 8
                            u = jnp.broadcast_to(unit[:, h * 2 + l : h * 2 + l + 1], (8, LANES))
                            exact[slot, at : at + 8, :] = code[l * 8 : l * 8 + 8] * u
                    reached = exact.at[slot]
                else:
                    reached = product_ref.at[p]
                retain = retain_ref[...]
                squared = retain * retain
                for c in range(samples):
                    i = p * samples + c
                    if inline:
                        own, gate = row_terms(*given[:4], retain_ref, given[4], order_ref[0, first + i])
                    for j in range(2):
                        at = slice(j * half, (j + 1) * half)
                        r = reached[pl.ds(c * 2 + j, half, stride=2 * samples), :]
                        mixed = (squared if j else retain) * r + (own[j] if inline else given[0][place + i, at, :])
                        out_ref[i, at, :] = mixed * (gate[j] if inline else given[1][place + i, at, :])
                        power = jnp.sum((mixed * mixed).reshape(half // 8, 8, LANES), axis=0)
                        power = jnp.sum(power, axis=1, keepdims=True)
                        totals[j] = jnp.where(lane == first + i, power, totals[j])
            return tuple(totals)

        totals = lax.fori_loop(0, prompts // 2, body, totals)
    for j, t in enumerate(totals):
        u = t + pltpu.roll(t, 4, 0)
        sum_ref[j * 8 : j * 8 + 8] = u + pltpu.roll(u, 2, 0) + sum_in[j * 8 : j * 8 + 8]


def combine(order, decay, sums, given, parts):
    lines = given[0].shape[1]
    products = [p[4] for p in parts]
    total = max(x.shape[1] if not p[0] else (x.shape[0] - 16) // p[2] for x, p in zip(products, parts))
    samples = total // lines
    outs = [jax.ShapeDtypeStruct((p[2] * samples, lines, LANES), jnp.float32) for p in parts]
    count = sum(p[2] for p in parts) * samples
    return pl.pallas_call(
        functools.partial(combine_kernel, tuple(p[:4] for p in parts), len(given) == 5),
        in_specs=[SMEM] + [VMEM] * (2 + len(given) + len(parts)),
        out_specs=[VMEM] * (len(parts) + 1),
        out_shape=[*outs, jax.ShapeDtypeStruct((16, LANES), jnp.float32)],
        scratch_shapes=[
            pltpu.VMEM((lines // 2, LANES), jnp.float32),
            pltpu.VMEM((16, LANES), jnp.float32),
            pltpu.VMEM((2, total, LANES), jnp.float32),
        ],
        compiler_params=params(16),
        cost_estimate=cost(0, count * lines * LANES * 14),
        name="combine",
    )(order, decay, sums, *given, *products)


def finish_kernel(features, first, splits, count, order_ref, *refs):
    tiles, refs = refs[:count], refs[count:]
    parts, (out_hbm, scratch, scale, sem) = refs[: len(splits)], refs[-4:]
    half = parts[0].shape[1] // 2
    total = sum(t[...] for t in tiles)
    scale[...] = lax.rsqrt(total / features + 1e-05)
    at = 0
    for part, rows in zip(parts, splits):

        def body(b, carry, part=part, at=at):
            turned = pltpu.roll(scale[...], lax.rem(2 * LANES - first - at - b * 8, LANES), 1)
            for i in range(8):
                row = b * 8 + i
                for j in range(2):
                    one = jnp.broadcast_to(turned[j * 8 : j * 8 + 8, i : i + 1], (8, LANES))
                    lines = part[row, j * half : (j + 1) * half, :].reshape(half // 8, 8, LANES)
                    scratch[at + row, j * half : (j + 1) * half, :] = (lines * one[None]).reshape(half, LANES)
                s = order_ref[0, first + at + row]
                pltpu.make_async_copy(scratch.at[at + row], out_hbm.at[s], sem).start()
            return carry

        lax.fori_loop(0, rows // 8, body, 0)
        at += rows
    pltpu.make_async_copy(scratch, out_hbm.at[pl.ds(0, at)], sem).wait()


def finish(order, tiles, parts, first, out, rows):
    splits = tuple(p.shape[0] for p in parts)
    lines = parts[0].shape[1]
    given = [order, *tiles, *parts] + ([] if out is None else [out])
    return pl.pallas_call(
        functools.partial(finish_kernel, HEADS * HEAD_DIM, first, splits, len(tiles)),
        in_specs=[SMEM] + [VMEM] * (len(tiles) + len(parts)) + ([] if out is None else [ANY]),
        out_specs=ANY,
        out_shape=jax.ShapeDtypeStruct((rows, lines, LANES), jnp.float32),
        scratch_shapes=[
            pltpu.VMEM((sum(splits), lines, LANES), jnp.float32),
            pltpu.VMEM((16, LANES), jnp.float32),
            pltpu.SemaphoreType.DMA,
        ],
        input_output_aliases={} if out is None else {len(given) - 1: 0},
        compiler_params=params(16),
        cost_estimate=cost(0, sum(splits) * lines * LANES * 8),
        name="finish",
    )(*given)


def local(
    prefill_states, prompt_slot, sample_prompt, queries, keys, values, gates, norm_gain, decay_rate
):
    group = lax.axis_index("dp")
    groups = lax.axis_size("dp")
    split = lax.axis_size("tensor")
    quarter = groups // 4
    owned = prefill_states.shape[0]
    rows, steps, layers, columns = queries.shape
    heads = columns // LANES
    per = rows // (4 * owned)
    lines = steps * layers * heads
    assert steps == 2 and layers == 2 and per * steps == 8 and rows <= LANES
    assert heads % 4 == 0 and heads * layers * owned <= 2 * LANES

    def swap(block, bits):
        far = [((i // quarter) ^ bits) * quarter + i % quarter for i in range(groups)]
        return lax.ppermute(block, "dp", [(f, i) for i, f in enumerate(far)])

    def shared(tile):
        if split not in (2, 4):
            return [lax.psum(tile, "tensor")]
        return [tile] + [
            lax.ppermute(tile, "tensor", [(i, i ^ k) for i in range(split)])
            for k in range(1, split)
        ]

    q, k, v, g = (rows_view(x) for x in (queries, keys, values, gates))
    gain = rows_view(norm_gain[None, None]).reshape(heads * layers, LANES)
    place = (group // quarter).astype(jnp.int32).reshape(1, 1)

    packed = jax.ShapeDtypeStruct((owned, per * lines, LANES), jnp.bfloat16)
    pack_scratch = pltpu.VMEM((2, per * lines, LANES), jnp.float32)
    order, near, next_ = pl.pallas_call(
        functools.partial(order_kernel, owned, quarter, (1, 2)),
        in_specs=[SMEM, ANY, ANY, ANY],
        out_specs=[SMEM, VMEM, VMEM],
        out_shape=[jax.ShapeDtypeStruct((1, rows), jnp.int32), packed, packed],
        scratch_shapes=[
            pltpu.VMEM(q.shape, q.dtype),
            pltpu.VMEM((1, prompt_slot.shape[0]), jnp.int32),
            pltpu.VMEM((1, rows), jnp.int32),
            pltpu.VMEM((1, rows), jnp.int32),
            pack_scratch,
            pltpu.SemaphoreType.DMA((4,)),
        ],
        compiler_params=params(60),
        cost_estimate=cost(0, 4 << 20),
        name="order",
    )(place, prompt_slot.reshape(1, -1), sample_prompt.reshape(1, -1), q)
    near, next_ = swap(near, 1), swap(next_, 2)
    chunk = owned * per
    ready = jax.ShapeDtypeStruct((chunk, lines, LANES), jnp.float32)
    far, mine, own, gate = pl.pallas_call(
        functools.partial(pack_kernel, per, owned, 3 * chunk),
        in_specs=[SMEM, VMEM, VMEM] + [ANY] * 4,
        out_specs=[VMEM, VMEM, ANY, ANY],
        out_shape=[packed, packed, ready, ready],
        scratch_shapes=[pltpu.VMEM(q.shape, q.dtype)] * 4
        + [pltpu.VMEM(ready.shape, jnp.float32)] * 2
        + [pltpu.VMEM(gain.shape, jnp.float32), pack_scratch, pltpu.SemaphoreType.DMA((12,))],
        compiler_params=params(BIG),
        cost_estimate=cost(0, 16 << 20),
        name="pack",
    )(order, decay_rate, gain, q, k, v, g)

    def after(value, *done):
        return lax.optimization_barrier((value, *done))[0]

    mine = reach(mine, prefill_states, 0, owned, False)
    far = swap(after(far, mine), 3)
    near_code = reach(after(near, mine), prefill_states, 0, owned, True)
    near = swap(near_code, 1)
    next_code = reach(after(next_, near_code), prefill_states, 0, owned, True)
    next_ = swap(next_code, 2)
    cuts = [owned // FAR * i for i in range(FAR + 1)]
    far_codes, code = [], next_code
    for begin, end in zip(cuts, cuts[1:]):
        code = reach(after(far, code), prefill_states, begin, end - begin, True)
        far_codes.append(swap(code, 3))

    zero = after(jnp.zeros((16, LANES), jnp.float32), code)
    sums, outs = zero, []
    for part in ((False, 0, owned, 0, mine), (True, chunk, owned, 0, near), (True, 2 * chunk, owned, 0, next_)):
        more, sums = combine(order, decay_rate, sums, (q, k, v, g, gain), [part])
        outs.append(more)
    early = shared(sums)
    sums, lates = zero, []
    for begin, end, x in zip(cuts, cuts[1:], far_codes):
        part = (True, 3 * chunk + begin * per, end - begin, begin * per, x)
        more, sums = combine(order, decay_rate, sums, (own, gate), [part])
        lates.append(more)
    late = shared(sums)
    out = finish(order, early, outs, 0, None, rows)
    out = finish(order, late, lates, 3 * chunk, out, rows)
    return rows_unview(out, steps, layers)


def solution(mesh):
    return jax.shard_map(
        local,
        mesh=mesh,
        in_specs=(
            P("dp", None, "tensor", None, None),
            P(),
            P("dp"),
            P("dp", None, None, "tensor"),
            P("dp", None, None, "tensor"),
            P("dp", None, None, "tensor"),
            P("dp", None, None, "tensor"),
            P(None, "tensor"),
            P(None, "tensor"),
        ),
        out_specs=P("dp", None, None, "tensor"),
        check_vma=False,
    )
```

time: 153 us -> 69 us (0.45)
  local copies, waits for them, and re-layouts: 43.3 us -> 1.09 us
  Pallas kernels: 0 us -> 34.3 us
  other arithmetic: 29.5 us -> 0 us
  waiting for transfers between devices: 37 us -> 13 us
  matrix products: 22.7 us -> 0 us
  starting transfers between devices: 7.98 us -> 20.2 us
  blocking collectives: 11.9 us -> 0 us
    pallas_call x0 -> x14, Pallas kernels: none -> 34.3 us  [the longest x5 10.8 us: combine(): pl.pallas_call(functools.partial(combine_kernel, tuple((p[:4] for p in pa...]
    ppermute x6 -> x13, waiting for transfers between devices: 37 us -> 13 us  [the longest x7 12.5 us: swap(): return lax.ppermute(block, 'dp', [(f, i) for i, f in enumerate(far)])]
    dot_general x4 -> x0, matrix products: 22.7 us -> none  [against(): jnp.einsum('psjlhd,plhde->psjlhe', query_block, states, preferred_element...]
    gather x2 -> x0, local copies, waits for them, and re-layouts: 14.1 us -> none  [the longest x1 9.19 us: local(): queries[order]]
    ppermute x6 -> x13, starting transfers between devices: 7.98 us -> 20.2 us  [the longest x7 11.1 us: swap(): return lax.ppermute(block, 'dp', [(f, i) for i, f in enumerate(far)])]
    psum x1 -> x0, blocking collectives: 11.9 us -> none  [local(): total = lax.psum(jnp.sum(mixed * mixed, axis=-1), 'tensor')]
    reshape x3 -> x0, local copies, waits for them, and re-layouts: 10.3 us -> none  [the longest x1 4.53 us: local(): key_all = keys.reshape(shape)]
    another operation x3 -> x0, local copies, waits for them, and re-layouts: 8.5 us -> none  [the longest x2 5.69 us: local(): jnp.stack([out_one, out_two], axis=1)]
  transfers between devices with their start and end apart: 6 -> 13, of which waited for: 3 -> 3; matrix products, arithmetic and copies ran while one was open for 29% -> 0% of each run, Pallas kernels for 0% -> 43%
where the time goes in v2:
time: 69 us; the launch traced here: 68.8 us
  Pallas kernels  34.3 us (50%)
  starting transfers between devices  20.2 us (29%)
  waiting for transfers between devices  13 us (19%)
  local copies, waits for them, and re-layouts  1.09 us (2%)
    ppermute x7, waiting for transfers between devices, swap(): return lax.ppermute(block, 'dp', [(f, i) for i, f in enumerate(far)])  12.5 us
    ppermute x7, starting transfers between devices, swap(): return lax.ppermute(block, 'dp', [(f, i) for i, f in enumerate(far)])  11.1 us
    pallas_call x5, Pallas kernels, combine(): pl.pallas_call(functools.partial(combine_kernel, tuple((p[:4] for p in pa...  10.8 us
    ppermute x6, starting transfers between devices, shared(): lax.ppermute(tile, 'tensor', [(i, i ^ k) for i in range(split)])  9.03 us
    pallas_call x1, Pallas kernels, local(): pl.pallas_call(functools.partial(pack_kernel, per, owned, 3 * chunk), in_...  8.07 us
    pallas_call x5, Pallas kernels, reach(): pl.pallas_call(functools.partial(reach_kernel, coded, begin, prompts), in...  7.23 us
    pallas_call x2, Pallas kernels, finish(): pl.pallas_call(functools.partial(finish_kernel, HEADS * HEAD_DIM, first,...  5.11 us
    pallas_call x1, Pallas kernels, local(): pl.pallas_call(functools.partial(order_kernel, owned, quarter, (1, 2)), i...  3.14 us
  transfers between devices with their start and end apart: 13, of which 3 were waited for; matrix products, arithmetic and copies ran while one was open for 0% of the time, Pallas kernels for 43%

profile of v2, /device:TPU:0, one launch (start us, length us, event | category | flops | bytes accessed | tf_op | source)
XLA Modules:
  0.0 68.8 jit_solution(3335919406477133758)
XLA Ops:
  0.0 3.1 %order.1 = (s32[1,128]{1,0:T(1,128)}, bf16[8,256,128]{2,1,0:T(8,128)(2,1)}, bf16[8,256,128]{2,1,0:T(8,128)(2,1)}) custom-call(s32[1,1]{1,0:T(1,128)} %bitcast.place_ref, s32[1,64]{1,0:T(1,128)} %bitcast.54, s32[1,128]{1,0:T(1,128)} %bitcast.55, bf16[128,64,128]{2,1,0:T(8,128)(2,1)} %bitcast.33), custom_call_target="tpu_custom_call" | custom-call | bytes 4194304 | tf_op jit(solution)/shard_map/order/pallas_call | solution.py:397
  3.2 3.0 %collective-permute-start.2 = (bf16[8,256,128]{2,1,0:T(8,128)(2,1)}, bf16[8,256,128]{2,1,0:T(8,128)(2,1)S(1)}, u32[]{:S(2)}, u32[]{:S(2)}) collective-permute-start(bf16[8,256,128]{2,1,0:T(8,128)(2,1)} %get-tuple-element.33), channel_id=1, source_target_pairs={{8,0},{12,4},{0,8},{4,12},{24,16},{28,20},{16,24},{20,28},{9,1},{1... | collective-permute-start | bytes 1572872 | tf_op jit(solution)/shard_map/ppermute | solution.py:381
  6.2 1.5 %collective-permute-start.1 = (bf16[8,256,128]{2,1,0:T(8,128)(2,1)}, bf16[8,256,128]{2,1,0:T(8,128)(2,1)S(1)}, u32[]{:S(2)}, u32[]{:S(2)}) collective-permute-start(bf16[8,256,128]{2,1,0:T(8,128)(2,1)} %get-tuple-element.32), channel_id=1, source_target_pairs={{16,0},{20,4},{24,8},{28,12},{0,16},{4,20},{8,24},{12,28},{17,1},{... | collective-permute-start | bytes 1572872 | tf_op jit(solution)/shard_map/ppermute | solution.py:381
  7.7 0.0 copy-start
  7.7 8.1 %pack.1 = (bf16[8,256,128]{2,1,0:T(8,128)(2,1)}, bf16[8,256,128]{2,1,0:T(8,128)(2,1)}, f32[32,64,128]{2,1,0:T(8,128)}, f32[32,64,128]{2,1,0:T(8,128)}) custom-call(s32[1,128]{1,0:T(1,128)} %get-tuple-element.28.order_ref, f32[2,16]{1,0:T(2,128)} %decay_ref.11, f32[32,128]{1,0:T(8,128)} %bitcast.50, bf16[128,64,128]{2,1,0:T(8,128)(2,1)} %bitcast.34, ...), custom_call_target="tpu_custom_call" | custom-call | bytes 16777216 | tf_op jit(solution)/shard_map/pack/pallas_call | solution.py:417
  15.8 0.0 copy-done
  15.8 0.0 copy-start.7
  15.8 1.0 %copy-done.7 = bf16[8,256,128]{2,1,0:T(8,128)(2,1)S(1)} copy-done((bf16[8,256,128]{2,1,0:T(8,128)(2,1)S(1)}, bf16[8,256,128]{2,1,0:T(8,128)(2,1)}, u32[]{:S(2)}) %copy-start.7) | copy-done | bytes 524312
  16.8 0.0 copy-start.11
  16.8 2.1 %reach.5.refs_5_ = f32[8,256,128]{2,1,0:T(8,128)S(1)} custom-call(bf16[8,256,128]{2,1,0:T(8,128)(2,1)S(1)} %copy-done.7, bf16[8,2,16,128,128]{4,3,2,1,0:T(8,128)(2,1)S(1)} %copy-done), custom_call_target="tpu_custom_call" | custom-call | flops 134217728 | bytes 8388608 | tf_op jit(solution)/shard_map/reach/pallas_call | solution.py:165
  18.9 0.0 copy-done.11
  18.9 0.1 collective-permute-start
  19.0 0.0 collective-permute-done.2.q_ref
  19.0 1.7 %reach.6 = s16[2064,128]{1,0:T(8,128)(2,1)S(1)} custom-call(bf16[8,256,128]{2,1,0:T(8,128)(2,1)S(1)} %collective-permute-done.2.q_ref, bf16[8,2,16,128,128]{4,3,2,1,0:T(8,128)(2,1)S(1)} %copy-done), custom_call_target="tpu_custom_call" | custom-call | flops 134217728 | bytes 8388608 | tf_op jit(solution)/shard_map/reach/pallas_call | solution.py:165
  20.7 2.0 %collective-permute-start.8 = (s16[2064,128]{1,0:T(8,128)(2,1)S(1)}, s16[2064,128]{1,0:T(8,128)(2,1)S(1)}, u32[]{:S(2)}, u32[]{:S(2)}) collective-permute-start(s16[2064,128]{1,0:T(8,128)(2,1)S(1)} %reach.6), channel_id=1, source_target_pairs={{8,0},{12,4},{0,8},{4,12},{24,16},{28,20},{16,24},{20,28},{9,1},{1... | collective-permute-start | bytes 1585160 | tf_op jit(solution)/shard_map/ppermute | solution.py:381
  22.7 0.0 collective-permute-done.1.q_ref
  22.7 1.7 %reach.7 = s16[2064,128]{1,0:T(8,128)(2,1)S(1)} custom-call(bf16[8,256,128]{2,1,0:T(8,128)(2,1)S(1)} %collective-permute-done.1.q_ref, bf16[8,2,16,128,128]{4,3,2,1,0:T(8,128)(2,1)S(1)} %copy-done), custom_call_target="tpu_custom_call" | custom-call | flops 134217728 | bytes 8388608 | tf_op jit(solution)/shard_map/reach/pallas_call | solution.py:165
  24.4 1.5 %collective-permute-start.9 = (s16[2064,128]{1,0:T(8,128)(2,1)S(1)}, s16[2064,128]{1,0:T(8,128)(2,1)S(1)}, u32[]{:S(2)}, u32[]{:S(2)}) collective-permute-start(s16[2064,128]{1,0:T(8,128)(2,1)S(1)} %reach.7), channel_id=1, source_target_pairs={{16,0},{20,4},{24,8},{28,12},{0,16},{4,20},{8,24},{12,28},{17,1},{... | collective-permute-start | bytes 1585160 | tf_op jit(solution)/shard_map/ppermute | solution.py:381
  26.0 8.7 %collective-permute-done.q_ref = bf16[8,256,128]{2,1,0:T(8,128)(2,1)S(1)} collective-permute-done((bf16[8,256,128]{2,1,0:T(8,128)(2,1)S(1)}, bf16[8,256,128]{2,1,0:T(8,128)(2,1)S(1)}, u32[]{:S(2)}, u32[]{:S(2)}) %collective-permute-start) | collective-permute-done | bytes 524320 | tf_op jit(solution)/shard_map/ppermute | solution.py:381
  34.7 0.8 %reach.8 = s16[1040,128]{1,0:T(8,128)(2,1)S(1)} custom-call(bf16[8,256,128]{2,1,0:T(8,128)(2,1)S(1)} %collective-permute-done.q_ref, bf16[8,2,16,128,128]{4,3,2,1,0:T(8,128)(2,1)S(1)} %copy-done), custom_call_target="tpu_custom_call" | custom-call | flops 67108864 | bytes 4194304 | tf_op jit(solution)/shard_map/reach/pallas_call | solution.py:165
  35.5 0.0 copy-start.1
  35.5 0.0 copy-start.2
  35.5 0.0 copy-start.3
  35.5 0.0 copy-start.4
  35.6 0.0 copy-start.8
  35.6 0.0 copy-start.9
  35.6 0.0 copy-start.10
  35.6 0.1 collective-permute-start.3
  35.7 0.8 %reach.9 = s16[1040,128]{1,0:T(8,128)(2,1)S(1)} custom-call(bf16[8,256,128]{2,1,0:T(8,128)(2,1)S(1)} %collective-permute-done.q_ref, bf16[8,2,16,128,128]{4,3,2,1,0:T(8,128)(2,1)S(1)} %copy-done), custom_call_target="tpu_custom_call" | custom-call | flops 67108864 | bytes 4194304 | tf_op jit(solution)/shard_map/reach/pallas_call | solution.py:165
  36.5 2.9 %collective-permute-start.4 = (s16[1040,128]{1,0:T(8,128)(2,1)S(1)}, s16[1040,128]{1,0:T(8,128)(2,1)S(1)}, u32[]{:S(2)}, u32[]{:S(2)}) collective-permute-start(s16[1040,128]{1,0:T(8,128)(2,1)S(1)} %reach.9), channel_id=1, source_target_pairs={{24,0},{28,4},{16,8},{20,12},{8,16},{12,20},{0,24},{4,28},{25,1},{... | collective-permute-start | bytes 798728 | tf_op jit(solution)/shard_map/ppermute | solution.py:381
  39.5 0.0 copy-done.1
  39.5 0.0 copy-done.2
  39.5 0.0 copy-done.3
  39.5 0.0 copy-done.4
  39.5 0.0 copy-done.8
  39.5 0.0 copy-done.9
  39.5 0.0 copy-done.10
  39.5 1.8 %combine.7 = (f32[32,64,128]{2,1,0:T(8,128)S(1)}, f32[16,128]{1,0:T(8,128)S(1)}) custom-call(s32[1,128]{1,0:T(1,128)S(1)} %copy-done.10, f32[2,16]{1,0:T(2,128)S(1)} %copy-done.9, f32[16,128]{1,0:T(8,128)S(1)} %broadcast_in_dim.3.sum_in, bf16[128,64,128]{2,1,0:T(8,128)(2,1)S(1)} %bitcast.35, bf16[128,64,128]{2,1,0:T(8,128)(2,1)S(1)} %bitcast.39, ...), custom_call_target="tpu_custom_call" | custom-call | bytes 3670016 | tf_op jit(solution)/shard_map/combine/pallas_call | solution.py:301
  41.3 3.8 %collective-permute-done.8.refs_5_ = s16[2064,128]{1,0:T(8,128)(2,1)S(1)} collective-permute-done((s16[2064,128]{1,0:T(8,128)(2,1)S(1)}, s16[2064,128]{1,0:T(8,128)(2,1)S(1)}, u32[]{:S(2)}, u32[]{:S(2)}) %collective-permute-start.8) | collective-permute-done | bytes 528416 | tf_op jit(solution)/shard_map/ppermute | solution.py:381
  45.1 3.1 %combine.8 = (f32[32,64,128]{2,1,0:T(8,128)S(1)}, f32[16,128]{1,0:T(8,128)S(1)}) custom-call(s32[1,128]{1,0:T(1,128)S(1)} %copy-done.10, f32[2,16]{1,0:T(2,128)S(1)} %copy-done.9, f32[16,128]{1,0:T(8,128)S(1)} %get-tuple-element.45.sum_in, bf16[128,64,128]{2,1,0:T(8,128)(2,1)S(1)} %bitcast.36, bf16[128,64,128]{2,1,0:T(8,128)(2,1)S(1)} %bitcast.40, ...), custom_call_target="tpu_custom_call" | custom-call | bytes 3670016 | tf_op jit(solution)/shard_map/combine/pallas_call | solution.py:301
  48.2 0.0 collective-permute-done.9.refs_5_
  48.2 0.0 copy-start.5
  48.2 0.0 copy-start.6
  48.2 3.1 %combine.9 = (f32[32,64,128]{2,1,0:T(8,128)S(1)}, f32[16,128]{1,0:T(8,128)S(1)}) custom-call(s32[1,128]{1,0:T(1,128)S(1)} %copy-done.10, f32[2,16]{1,0:T(2,128)S(1)} %copy-done.9, f32[16,128]{1,0:T(8,128)S(1)} %get-tuple-element.46.sum_in, bf16[128,64,128]{2,1,0:T(8,128)(2,1)S(1)} %bitcast.37, bf16[128,64,128]{2,1,0:T(8,128)(2,1)S(1)} %bitcast.41, ...), custom_call_target="tpu_custom_call" | custom-call | bytes 3670016 | tf_op jit(solution)/shard_map/combine/pallas_call | solution.py:301
  51.4 3.7 %collective-permute-start.12 = (f32[16,128]{1,0:T(8,128)S(1)}, f32[16,128]{1,0:T(8,128)S(1)}, u32[]{:S(2)}, u32[]{:S(2)}) collective-permute-start(f32[16,128]{1,0:T(8,128)S(1)} %get-tuple-element.47.refs_0_), channel_id=1, source_target_pairs={{0,3},{1,2},{2,1},{3,0},{4,7},{5,6},{6,5},{7,4},{8,11},{9,10},{10,... | collective-permute-start | bytes 24584 | tf_op jit(solution)/shard_map/ppermute | solution.py:387
  55.0 0.0 collective-permute-done.3.refs_2_
  55.0 0.0 copy-done.5
  55.0 0.0 copy-done.6
  55.0 1.4 %combine.5 = (f32[16,64,128]{2,1,0:T(8,128)S(1)}, f32[16,128]{1,0:T(8,128)S(1)}) custom-call(s32[1,128]{1,0:T(1,128)S(1)} %copy-done.10, f32[2,16]{1,0:T(2,128)S(1)} %copy-done.9, f32[16,128]{1,0:T(8,128)S(1)} %broadcast_in_dim.3.sum_in, f32[32,64,128]{2,1,0:T(8,128)S(1)} %copy-done.5, f32[32,64,128]{2,1,0:T(8,128)S(1)} %copy-done.6, ...), custom_call_target="tpu_custom_call" | custom-call | bytes 1835008 | tf_op jit(solution)/shard_map/combine/pallas_call | solution.py:301
  56.4 0.1 collective-permute-start.11
  56.5 0.8 %collective-permute-start.10 = (f32[16,128]{1,0:T(8,128)S(1)}, f32[16,128]{1,0:T(8,128)S(1)}, u32[]{:S(2)}, u32[]{:S(2)}) collective-permute-start(f32[16,128]{1,0:T(8,128)S(1)} %get-tuple-element.47.refs_0_), channel_id=1, source_target_pairs={{0,1},{1,0},{2,3},{3,2},{4,5},{5,4},{6,7},{7,6},{8,9},{9,8},{10,11... | collective-permute-start | bytes 24584 | tf_op jit(solution)/shard_map/ppermute | solution.py:387
  57.3 0.0 collective-permute-done.4.refs_2_
  57.3 1.4 %combine.6 = (f32[16,64,128]{2,1,0:T(8,128)S(1)}, f32[16,128]{1,0:T(8,128)S(1)}) custom-call(s32[1,128]{1,0:T(1,128)S(1)} %copy-done.10, f32[2,16]{1,0:T(2,128)S(1)} %copy-done.9, f32[16,128]{1,0:T(8,128)S(1)} %get-tuple-element.41.sum_in, f32[32,64,128]{2,1,0:T(8,128)S(1)} %copy-done.5, f32[32,64,128]{2,1,0:T(8,128)S(1)} %copy-done.6, ...), custom_call_target="tpu_custom_call" | custom-call | bytes 1835008 | tf_op jit(solution)/shard_map/combine/pallas_call | solution.py:301
  58.7 3.6 %collective-permute-start.7 = (f32[16,128]{1,0:T(8,128)S(1)}, f32[16,128]{1,0:T(8,128)S(1)}, u32[]{:S(2)}, u32[]{:S(2)}) collective-permute-start(f32[16,128]{1,0:T(8,128)S(1)} %get-tuple-element.42.refs_0_), channel_id=1, source_target_pairs={{0,3},{1,2},{2,1},{3,0},{4,7},{5,6},{6,5},{7,4},{8,11},{9,10},{10,... | collective-permute-start | bytes 24584 | tf_op jit(solution)/shard_map/ppermute | solution.py:387
  62.3 0.0 collective-permute-start.6
  62.3 0.0 collective-permute-done.12.refs_3_
  62.3 0.8 %collective-permute-start.5 = (f32[16,128]{1,0:T(8,128)S(1)}, f32[16,128]{1,0:T(8,128)S(1)}, u32[]{:S(2)}, u32[]{:S(2)}) collective-permute-start(f32[16,128]{1,0:T(8,128)S(1)} %get-tuple-element.42.refs_0_), channel_id=1, source_target_pairs={{0,1},{1,0},{2,3},{3,2},{4,5},{5,4},{6,7},{7,6},{8,9},{9,8},{10,11... | collective-permute-start | bytes 24584 | tf_op jit(solution)/shard_map/ppermute | solution.py:387
  63.2 0.0 collective-permute-done.11.refs_2_
  63.2 0.0 collective-permute-done.10.refs_1_
  63.2 3.2 %finish.2.refs_6_ = f32[128,64,128]{2,1,0:T(8,128)} custom-call(s32[1,128]{1,0:T(1,128)S(1)} %copy-done.10, f32[16,128]{1,0:T(8,128)S(1)} %get-tuple-element.47.refs_0_, f32[16,128]{1,0:T(8,128)S(1)} %collective-permute-done.10.refs_1_, f32[16,128]{1,0:T(8,128)S(1)} %collective-permute-done.11.refs_2_, f32[16,128]{1,0:T(8,128)S(1)} %collective-permute-done.12.refs_3_, ...), custom_call_target="tpu_custom_call" | custom-call | bytes 6291456 | tf_op jit(solution)/shard_map/finish/pallas_call | solution.py:347
  66.4 0.0 collective-permute-done.7.refs_3_
  66.4 0.4 collective-permute-done.6.refs_2_
  66.9 0.0 collective-permute-done.5.refs_1_
  66.9 1.9 %finish.3 = f32[128,64,128]{2,1,0:T(8,128)} custom-call(s32[1,128]{1,0:T(1,128)S(1)} %copy-done.10, f32[16,128]{1,0:T(8,128)S(1)} %get-tuple-element.42.refs_0_, f32[16,128]{1,0:T(8,128)S(1)} %collective-permute-done.5.refs_1_, f32[16,128]{1,0:T(8,128)S(1)} %collective-permute-done.6.refs_2_, ...), custom_call_target="tpu_custom_call", output_to_operand_aliasing={{}: (7, {})} | custom-call | bytes 2097152 | tf_op jit(solution)/shard_map/finish/pallas_call | solution.py:347
  (1 shorter events, 0.0 us)
Async XLA Ops:
  3.2 15.8 %collective-permute-start.2 = (bf16[8,256,128]{2,1,0:T(8,128)(2,1)}, bf16[8,256,128]{2,1,0:T(8,128)(2,1)S(1)}, u32[]{:S(2)}, u32[]{:S(2)}) collective-permute-start(bf16[8,256,128]{2,1,0:T(8,128)(2,1)} %get-tuple-element.33), channel_id=1, source_target_pairs={{8,0},{12,4},{0,8},{4,12},{24,16},{28,20},{16,24},{20,28},{9,1},{1... | collective-permute-start | bytes 1572872 | tf_op jit(solution)/shard_map/ppermute | solution.py:381
  6.2 16.5 %collective-permute-start.1 = (bf16[8,256,128]{2,1,0:T(8,128)(2,1)}, bf16[8,256,128]{2,1,0:T(8,128)(2,1)S(1)}, u32[]{:S(2)}, u32[]{:S(2)}) collective-permute-start(bf16[8,256,128]{2,1,0:T(8,128)(2,1)} %get-tuple-element.32), channel_id=1, source_target_pairs={{16,0},{20,4},{24,8},{28,12},{0,16},{4,20},{8,24},{12,28},{17,1},{... | collective-permute-start | bytes 1572872 | tf_op jit(solution)/shard_map/ppermute | solution.py:381
  7.7 8.1 %copy-start = (bf16[8,2,16,128,128]{4,3,2,1,0:T(8,128)(2,1)S(1)}, bf16[8,2,16,128,128]{4,3,2,1,0:T(8,128)(2,1)}, u32[]{:S(2)}) copy-start(bf16[8,2,16,128,128]{4,3,2,1,0:T(8,128)(2,1)} %s_ref.9) | copy-start | bytes 25165828
  15.8 1.0 %copy-start.7 = (bf16[8,256,128]{2,1,0:T(8,128)(2,1)S(1)}, bf16[8,256,128]{2,1,0:T(8,128)(2,1)}, u32[]{:S(2)}) copy-start(bf16[8,256,128]{2,1,0:T(8,128)(2,1)} %get-tuple-element.30.q_ref) | copy-start | bytes 1572868
  16.8 2.1 %copy-start.11 = (bf16[8,256,128]{2,1,0:T(8,128)(2,1)S(1)}, bf16[8,256,128]{2,1,0:T(8,128)(2,1)}, u32[]{:S(2)}) copy-start(bf16[8,256,128]{2,1,0:T(8,128)(2,1)} %get-tuple-element.31) | copy-start | bytes 1572868
  18.9 15.8 %collective-permute-start = (bf16[8,256,128]{2,1,0:T(8,128)(2,1)S(1)}, bf16[8,256,128]{2,1,0:T(8,128)(2,1)S(1)}, u32[]{:S(2)}, u32[]{:S(2)}) collective-permute-start(bf16[8,256,128]{2,1,0:T(8,128)(2,1)S(1)} %copy-done.11), channel_id=1, source_target_pairs={{24,0},{28,4},{16,8},{20,12},{8,16},{12,20},{0,24},{4,28},{25,1},{... | collective-permute-start | bytes 1572872 | tf_op jit(solution)/shard_map/ppermute | solution.py:381
  20.7 24.3 %collective-permute-start.8 = (s16[2064,128]{1,0:T(8,128)(2,1)S(1)}, s16[2064,128]{1,0:T(8,128)(2,1)S(1)}, u32[]{:S(2)}, u32[]{:S(2)}) collective-permute-start(s16[2064,128]{1,0:T(8,128)(2,1)S(1)} %reach.6), channel_id=1, source_target_pairs={{8,0},{12,4},{0,8},{4,12},{24,16},{28,20},{16,24},{20,28},{9,1},{1... | collective-permute-start | bytes 1585160 | tf_op jit(solution)/shard_map/ppermute | solution.py:381
  24.4 23.8 %collective-permute-start.9 = (s16[2064,128]{1,0:T(8,128)(2,1)S(1)}, s16[2064,128]{1,0:T(8,128)(2,1)S(1)}, u32[]{:S(2)}, u32[]{:S(2)}) collective-permute-start(s16[2064,128]{1,0:T(8,128)(2,1)S(1)} %reach.7), channel_id=1, source_target_pairs={{16,0},{20,4},{24,8},{28,12},{0,16},{4,20},{8,24},{12,28},{17,1},{... | collective-permute-start | bytes 1585160 | tf_op jit(solution)/shard_map/ppermute | solution.py:381
  35.5 3.9 %copy-start.1 = (bf16[128,2,2,2048]{3,2,1,0:T(2,128)(2,1)S(1)}, bf16[128,2,2,2048]{3,2,1,0:T(2,128)(2,1)}, u32[]{:S(2)}) copy-start(bf16[128,2,2,2048]{3,2,1,0:T(2,128)(2,1)} %param.12) | copy-start | bytes 6291460
  35.5 3.9 %copy-start.2 = (bf16[128,2,2,2048]{3,2,1,0:T(2,128)(2,1)S(1)}, bf16[128,2,2,2048]{3,2,1,0:T(2,128)(2,1)}, u32[]{:S(2)}) copy-start(bf16[128,2,2,2048]{3,2,1,0:T(2,128)(2,1)} %param.13) | copy-start | bytes 6291460
  35.5 3.9 %copy-start.3 = (bf16[128,2,2,2048]{3,2,1,0:T(2,128)(2,1)S(1)}, bf16[128,2,2,2048]{3,2,1,0:T(2,128)(2,1)}, u32[]{:S(2)}) copy-start(bf16[128,2,2,2048]{3,2,1,0:T(2,128)(2,1)} %param.14) | copy-start | bytes 6291460
  35.5 3.9 %copy-start.4 = (bf16[128,2,2,2048]{3,2,1,0:T(2,128)(2,1)S(1)}, bf16[128,2,2,2048]{3,2,1,0:T(2,128)(2,1)}, u32[]{:S(2)}) copy-start(bf16[128,2,2,2048]{3,2,1,0:T(2,128)(2,1)} %param.15) | copy-start | bytes 6291460
  35.6 3.9 %copy-start.8 = (f32[2,2048]{1,0:T(2,128)S(1)}, f32[2,2048]{1,0:T(2,128)}, u32[]{:S(2)}) copy-start(f32[2,2048]{1,0:T(2,128)} %param.16) | copy-start | bytes 49156
  35.6 3.9 %copy-start.9 = (f32[2,16]{1,0:T(2,128)S(1)}, f32[2,16]{1,0:T(2,128)}, u32[]{:S(2)}) copy-start(f32[2,16]{1,0:T(2,128)} %decay_ref.11) | copy-start | bytes 388
  35.6 3.9 %copy-start.10 = (s32[1,128]{1,0:T(1,128)S(1)}, s32[1,128]{1,0:T(1,128)}, u32[]{:S(2)}) copy-start(s32[1,128]{1,0:T(1,128)} %get-tuple-element.28.order_ref) | copy-start | bytes 1540
  35.6 19.4 %collective-permute-start.3 = (s16[1040,128]{1,0:T(8,128)(2,1)S(1)}, s16[1040,128]{1,0:T(8,128)(2,1)S(1)}, u32[]{:S(2)}, u32[]{:S(2)}) collective-permute-start(s16[1040,128]{1,0:T(8,128)(2,1)S(1)} %reach.8), channel_id=1, source_target_pairs={{24,0},{28,4},{16,8},{20,12},{8,16},{12,20},{0,24},{4,28},{25,1},{... | collective-permute-start | bytes 798728 | tf_op jit(solution)/shard_map/ppermute | solution.py:381
  36.5 20.8 %collective-permute-start.4 = (s16[1040,128]{1,0:T(8,128)(2,1)S(1)}, s16[1040,128]{1,0:T(8,128)(2,1)S(1)}, u32[]{:S(2)}, u32[]{:S(2)}) collective-permute-start(s16[1040,128]{1,0:T(8,128)(2,1)S(1)} %reach.9), channel_id=1, source_target_pairs={{24,0},{28,4},{16,8},{20,12},{8,16},{12,20},{0,24},{4,28},{25,1},{... | collective-permute-start | bytes 798728 | tf_op jit(solution)/shard_map/ppermute | solution.py:381
  48.2 6.8 %copy-start.5 = (f32[32,64,128]{2,1,0:T(8,128)S(1)}, f32[32,64,128]{2,1,0:T(8,128)}, u32[]{:S(2)}) copy-start(f32[32,64,128]{2,1,0:T(8,128)} %get-tuple-element.39.refs_0_) | copy-start | bytes 3145732
  48.2 6.8 %copy-start.6 = (f32[32,64,128]{2,1,0:T(8,128)S(1)}, f32[32,64,128]{2,1,0:T(8,128)}, u32[]{:S(2)}) copy-start(f32[32,64,128]{2,1,0:T(8,128)} %get-tuple-element.40.refs_1_) | copy-start | bytes 3145732
  51.4 11.0 %collective-permute-start.12 = (f32[16,128]{1,0:T(8,128)S(1)}, f32[16,128]{1,0:T(8,128)S(1)}, u32[]{:S(2)}, u32[]{:S(2)}) collective-permute-start(f32[16,128]{1,0:T(8,128)S(1)} %get-tuple-element.47.refs_0_), channel_id=1, source_target_pairs={{0,3},{1,2},{2,1},{3,0},{4,7},{5,6},{6,5},{7,4},{8,11},{9,10},{10,... | collective-permute-start | bytes 24584 | tf_op jit(solution)/shard_map/ppermute | solution.py:387
  56.4 6.8 %collective-permute-start.11 = (f32[16,128]{1,0:T(8,128)S(1)}, f32[16,128]{1,0:T(8,128)S(1)}, u32[]{:S(2)}, u32[]{:S(2)}) collective-permute-start(f32[16,128]{1,0:T(8,128)S(1)} %get-tuple-element.47.refs_0_), channel_id=1, source_target_pairs={{0,2},{1,3},{2,0},{3,1},{4,6},{5,7},{6,4},{7,5},{8,10},{9,11},{10,... | collective-permute-start | bytes 24584 | tf_op jit(solution)/shard_map/ppermute | solution.py:387
  56.5 6.7 %collective-permute-start.10 = (f32[16,128]{1,0:T(8,128)S(1)}, f32[16,128]{1,0:T(8,128)S(1)}, u32[]{:S(2)}, u32[]{:S(2)}) collective-permute-start(f32[16,128]{1,0:T(8,128)S(1)} %get-tuple-element.47.refs_0_), channel_id=1, source_target_pairs={{0,1},{1,0},{2,3},{3,2},{4,5},{5,4},{6,7},{7,6},{8,9},{9,8},{10,11... | collective-permute-start | bytes 24584 | tf_op jit(solution)/shard_map/ppermute | solution.py:387
  58.7 7.7 %collective-permute-start.7 = (f32[16,128]{1,0:T(8,128)S(1)}, f32[16,128]{1,0:T(8,128)S(1)}, u32[]{:S(2)}, u32[]{:S(2)}) collective-permute-start(f32[16,128]{1,0:T(8,128)S(1)} %get-tuple-element.42.refs_0_), channel_id=1, source_target_pairs={{0,3},{1,2},{2,1},{3,0},{4,7},{5,6},{6,5},{7,4},{8,11},{9,10},{10,... | collective-permute-start | bytes 24584 | tf_op jit(solution)/shard_map/ppermute | solution.py:387
  62.3 4.5 %collective-permute-start.6 = (f32[16,128]{1,0:T(8,128)S(1)}, f32[16,128]{1,0:T(8,128)S(1)}, u32[]{:S(2)}, u32[]{:S(2)}) collective-permute-start(f32[16,128]{1,0:T(8,128)S(1)} %get-tuple-element.42.refs_0_), channel_id=1, source_target_pairs={{0,2},{1,3},{2,0},{3,1},{4,6},{5,7},{6,4},{7,5},{8,10},{9,11},{10,... | collective-permute-start | bytes 24584 | tf_op jit(solution)/shard_map/ppermute | solution.py:387
  62.3 4.5 %collective-permute-start.5 = (f32[16,128]{1,0:T(8,128)S(1)}, f32[16,128]{1,0:T(8,128)S(1)}, u32[]{:S(2)}, u32[]{:S(2)}) collective-permute-start(f32[16,128]{1,0:T(8,128)S(1)} %get-tuple-element.42.refs_0_), channel_id=1, source_target_pairs={{0,1},{1,0},{2,3},{3,2},{4,5},{5,4},{6,7},{7,6},{8,9},{9,8},{10,11... | collective-permute-start | bytes 24584 | tf_op jit(solution)/shard_map/ppermute | solution.py:387
